TPU v7x, 256 devices: a whole 4x4x8 slice. The times are simulated.
256 devices in a mesh: section: 32 (over y, z_lo, core), dp: 8 (over z_hi, x).
Axes of the slice: x: 4, y: 4, z: 8 (z_hi: 2, z_lo: 4; z = z_hi * 4 + z_lo), core: 2. Of those that a mesh axis runs over, the one named last changes fastest.
Arguments:
- activations: bfloat16 [2, 32, 8, 8, 32, 416], P(None, 'section', 'dp'), may hold values from -6 to 6
- stored_inputs: bfloat16 [2, 3, 32, 8, 8, 32, 416], P(None, None, 'section', 'dp'), may hold values from -6 to 6
- cotangents: bfloat16 [2, 32, 8, 8, 32, 416], P(None, 'section', 'dp'), may hold values from -6 to 6
- new_inputs: bfloat16 [2, 2, 8, 8, 32, 416], P(None, None, 'dp'), may hold values from -6 to 6
- loss_grad: bfloat16 [2, 2, 8, 8, 32, 416], P(None, None, 'dp'), may hold values from -6 to 6
- depth_kernel: bfloat16 [32, 2, 1, 5, 5, 416], P('section'), may hold values from -1.25 to 1.25
- depth_bias: float32 [32, 2, 1, 416], P('section'), may hold values from -3 to 3
- mixing: bfloat16 [32, 2, 1, 416, 416], P('section'), may hold values from -0.3125 to 0.3125
Outputs:
- section_outputs: bfloat16 [2, 32, 8, 8, 32, 416], P(None, 'section', 'dp')
- input_grads: bfloat16 [2, 32, 8, 8, 32, 416], P(None, 'section', 'dp')
- grad_kernel: float32 [32, 1, 5, 5, 416], P('section', None, None, None, 'dp')
- grad_bias: float32 [32, 1, 416], P('section', None, 'dp')
- grad_mixing: float32 [32, 1, 416, 416], P('section', None, 'dp')
All inputs are finite; a program needn't handle non-finite values.
Results may differ from a plain program's by a relative error of at most 0.0062.
Values may be sent and summed in bfloat16 or wider, within the bound.
No kernel may reach another device: no remote copies, remote signals or barrier semaphores. Data moves between devices by JAX's collectives and lax.ppermute only.
A program may use at most 128 MiB of HBM per device.

v0:
```python
import functools

import jax
import jax.numpy as jnp
from jax import lax
from jax.experimental import pallas as pl
from jax.experimental.pallas import tpu as pltpu
from jax.sharding import PartitionSpec as P

F32 = jnp.float32
BF16 = jnp.bfloat16
LANES = 128
SUB = 8
SLOPE = 0.7978845608028654
CUBE = 0.044715


def tiles_of(channels):
    return -(-channels // LANES)


def span_of(tile, channels):
    return min(LANES, channels - tile * LANES)


def clear_margins(pad_ref, channels):
    tiles, height, rows, _ = pad_ref.shape
    zero = jnp.zeros((SUB, LANES), F32)
    for tile in range(tiles):
        full = span_of(tile, channels) < LANES
        for row in range(height):
            starts = range(0, rows, SUB) if full else (0, rows - SUB)
            for start in starts:
                pad_ref[tile, row, pl.ds(start, SUB), :] = zero


def fill(pad_ref, row, block, channels):
    width = block.shape[0]
    for tile in range(pad_ref.shape[0]):
        span = span_of(tile, channels)
        pad_ref[tile, row, pl.ds(SUB, width), 0:span] = block[:, tile * LANES : tile * LANES + span]


def load_params(kernel_ref, bias_ref, replica, taps_ref, shift_ref, channels):
    side = kernel_ref.shape[3]
    tiles = taps_ref.shape[0]
    taps_ref[tiles - 1] = jnp.zeros(taps_ref.shape[1:], F32)
    if shift_ref is not None:
        shift_ref[tiles - 1] = jnp.zeros(shift_ref.shape[1:], F32)
    for tap_row in range(side):
        rows = kernel_ref[0, replica, 0, tap_row].astype(F32)
        for tile in range(tiles):
            span = span_of(tile, channels)
            taps_ref[tile, pl.ds(tap_row * side, side), 0:span] = rows[:, tile * LANES : tile * LANES + span]
    if shift_ref is not None:
        rows = bias_ref[0, replica]
        for tile in range(tiles):
            span = span_of(tile, channels)
            shift_ref[tile, 0:1, 0:span] = rows[:, tile * LANES : tile * LANES + span]


def spread(ref, tile, row):
    return jnp.broadcast_to(ref[tile, pl.ds(row, 1), :], (SUB, LANES))


def conv_tile(pad_ref, taps_ref, tile, side, flip, emit):
    margin = side // 2
    height = pad_ref.shape[1]
    width = pad_ref.shape[2] - 2 * SUB
    last = side * side - 1
    taps = [
        [spread(taps_ref, tile, last - (a * side + b) if flip else a * side + b) for b in range(side)]
        for a in range(side)
    ]
    for start in range(0, width, SUB):
        running = {}
        for source in range(height):
            window = [pad_ref[tile, source, pl.ds(SUB + start - margin + b, SUB), :] for b in range(side)]
            for a in range(side):
                row = source - (a - margin)
                if 0 <= row < height:
                    for b in range(side):
                        term = taps[a][b] * window[b]
                        running[row] = running[row] + term if row in running else term
            done = [r for r in sorted(running) if r + margin <= source or source == height - 1]
            for row in done:
                emit(row, start, running.pop(row))


def tap_grads(pad_ref, grad_ref, tile, side, acc_ref):
    margin = side // 2
    height = pad_ref.shape[1]
    width = pad_ref.shape[2] - 2 * SUB
    sums = [None] * (side * side)
    total = None
    for start in range(0, width, SUB):
        held = {}
        for source in range(height):
            window = [pad_ref[tile, source, pl.ds(SUB + start - margin + b, SUB), :] for b in range(side)]
            for a in range(side):
                row = source - (a - margin)
                if 0 <= row < height:
                    if row not in held:
                        held[row] = grad_ref[tile, row, pl.ds(SUB + start, SUB), :]
                        total = held[row] if total is None else total + held[row]
                    for b in range(side):
                        term = held[row] * window[b]
                        at = a * side + b
                        sums[at] = term if sums[at] is None else sums[at] + term
            held.pop(source - margin, None)
    for at, value in enumerate(sums + [total]):
        acc_ref[tile, pl.ds(at, 1), :] = jnp.sum(value, axis=0, keepdims=True)


def gelu_parts(u, slope):
    square = u * u
    t = jnp.tanh(u * (SLOPE + (SLOPE * CUBE) * square))
    half = 0.5 * (1.0 + t)
    hidden = u * half
    if not slope:
        return hidden, None
    rate = half + hidden * (1.0 - t) * (SLOPE + (3.0 * SLOPE * CUBE) * square)
    return hidden, rate


def activate(pad_ref, taps_ref, shift_ref, side, act_ref, rate_ref, rate_at):
    def body(tile, carry):
        shift = spread(shift_ref, tile, 0)

        def emit(row, start, value):
            hidden, rate = gelu_parts(value + shift, rate_ref is not None)
            act_ref[tile, row, pl.ds(start, SUB), :] = hidden
            if rate_ref is not None:
                rate_ref[rate_at + (tile, row, pl.ds(start, SUB))] = rate

        conv_tile(pad_ref, taps_ref, tile, side, False, emit)
        return carry

    lax.fori_loop(0, pad_ref.shape[0], body, 0)


def pack_hidden(act_ref, hid_ref, hid_at, channels):
    tiles, height, width, _ = act_ref.shape
    for tile in range(tiles):
        span = span_of(tile, channels)
        for row in range(height):
            hid_ref[hid_at + (pl.ds(row * width, width), pl.ds(tile * LANES, span))] = act_ref[
                tile, row, :, 0:span
            ].astype(BF16)


def run_forward(read, params, replica, scratch, write, channels, side):
    kernel_ref, bias_ref, mixing_ref = params
    pad_ref, taps_ref, shift_ref, act_ref, hid_ref = scratch
    height, width = act_ref.shape[1:3]
    load_params(kernel_ref, bias_ref, replica, taps_ref, shift_ref, channels)
    for row in range(height):
        fill(pad_ref, row, read(row).astype(F32), channels)
    activate(pad_ref, taps_ref, shift_ref, side, act_ref, None, None)
    pack_hidden(act_ref, hid_ref, (), channels)
    mixed = jnp.dot(hid_ref[...], mixing_ref[0, replica, 0], preferred_element_type=F32)
    for row in range(height):
        write(row, (read(row).astype(F32) + mixed[row * width : (row + 1) * width]).astype(BF16))


def run_recompute(stored_ref, params, replica, scratch, hid_ref, hid_at, rate_ref, rate_at, channels, side):
    kernel_ref, bias_ref, _ = params
    pad_ref, taps_ref, shift_ref, act_ref = scratch
    height = act_ref.shape[1]
    load_params(kernel_ref, bias_ref, replica, taps_ref, shift_ref, channels)
    for row in range(height):
        fill(pad_ref, row, stored_ref[replica, 0, 0, 0, row].astype(F32), channels)
    activate(pad_ref, taps_ref, shift_ref, side, act_ref, rate_ref, rate_at)
    pack_hidden(act_ref, hid_ref, hid_at, channels)


def run_backward(read, params, replica, pads, taps_ref, work, rate_ref, rate_at, write, acc_ref, channels, side):
    _, _, mixing_ref = params
    pad_ref, slope_ref = pads
    back_ref, dx_ref, flat_ref = work
    tiles, height, width, _ = dx_ref.shape
    for row in range(height):
        flat_ref[pl.ds(row * width, width), :] = read(row)
    back_ref[:, 0:channels] = lax.dot_general(
        flat_ref[...], mixing_ref[0, replica, 0], (((1,), (1,)), ((), ())), preferred_element_type=F32
    )
    for tile in range(tiles):
        for row in range(height):
            slope_ref[tile, row, pl.ds(SUB, width), :] = (
                back_ref[pl.ds(row * width, width), pl.ds(tile * LANES, LANES)] * rate_ref[rate_at + (tile, row)]
            )

    def body(tile, carry):
        def emit(row, start, value):
            dx_ref[tile, row, pl.ds(start, SUB), :] = value

        conv_tile(slope_ref, taps_ref, tile, side, True, emit)
        tap_grads(pad_ref, slope_ref, tile, side, acc_ref)
        return carry

    lax.fori_loop(0, tiles, body, 0)
    for row in range(height):
        for tile in range(tiles):
            span = span_of(tile, channels)
            write(
                row,
                tile,
                span,
                (
                    dx_ref[tile, row, :, 0:span]
                    + flat_ref[pl.ds(row * width, width), pl.ds(tile * LANES, span)].astype(F32)
                ).astype(BF16),
            )


def mix_grad(hid_ref, flat_ref):
    return lax.dot_general(hid_ref, flat_ref, (((0,), (0,)), ((), ())), preferred_element_type=F32)


def writer(ref, lead):
    def write(row, tile, span, block):
        ref[lead + (row, slice(None), pl.ds(tile * LANES, span))] = block

    return write


def first_backward(channels, side, stored_ref, cot_ref, kernel_ref, bias_ref, mixing_ref,
                   gxa_ref, gxb_ref, hid_ref, acc_ref,
                   pad_ref, slope_ref, taps_ref, shift_ref, act_ref, rate_ref, back_ref, dx_ref, flat_ref):
    params = (kernel_ref, bias_ref, mixing_ref)
    clear_margins(pad_ref, channels)
    clear_margins(slope_ref, channels)
    back_ref[:, pl.ds((back_ref.shape[1] // LANES - 1) * LANES, LANES)] = jnp.zeros((back_ref.shape[0], LANES), F32)
    for replica, out_ref in ((0, gxa_ref), (1, gxb_ref)):
        run_recompute(stored_ref, params, replica, (pad_ref, taps_ref, shift_ref, act_ref),
                      hid_ref, (replica,), rate_ref, (), channels, side)
        run_backward(lambda row: cot_ref[replica, 0, 0, row], params, replica, (pad_ref, slope_ref), taps_ref,
                     (back_ref, dx_ref, flat_ref), rate_ref, (), writer(out_ref, ()), acc_ref.at[replica], channels, side)


def forward_recompute(channels, side, entering, *refs):
    refs = list(refs)
    if entering:
        recv_a_ref, recv_b_ref, new_ref = refs[:3]
        refs = refs[3:]
        at_start = lax.axis_index("section") == 0
        at_end = lax.axis_index("section") == lax.axis_size("section") - 1

        def reader(replica):
            flag, ref = ((at_start, recv_a_ref), (at_end, recv_b_ref))[replica]
            return lambda row: jnp.where(flag, new_ref[replica, 0, 0, row].astype(F32), ref[row].astype(F32)).astype(BF16)
    else:
        act_in_ref = refs[0]
        refs = refs[1:]

        def reader(replica):
            return lambda row: act_in_ref[replica, 0, 0, row]

    (stored_ref, kernel_ref, bias_ref, mixing_ref, fa_ref, fb_ref, hid_ref, rate_ref,
     pad_ref, taps_ref, shift_ref, act_ref, mid_ref, x_ref) = refs
    params = (kernel_ref, bias_ref, mixing_ref)
    clear_margins(pad_ref, channels)
    for replica, out_ref in ((0, fa_ref), (1, fb_ref)):
        read = reader(replica)
        for row in range(x_ref.shape[0]):
            x_ref[row] = read(row)

        def write(row, block):
            out_ref[row] = block

        run_forward(lambda row: x_ref[row], params, replica, (pad_ref, taps_ref, shift_ref, act_ref, mid_ref), write,
                    channels, side)
        run_recompute(stored_ref, params, replica, (pad_ref, taps_ref, shift_ref, act_ref),
                      hid_ref, (replica,), rate_ref, (replica,), channels, side)


def last_forward(channels, side, recv_a_ref, recv_b_ref, new_ref, kernel_ref, bias_ref, mixing_ref, out_ref,
                 pad_ref, taps_ref, shift_ref, act_ref, mid_ref, x_ref):
    params = (kernel_ref, bias_ref, mixing_ref)
    clear_margins(pad_ref, channels)
    at_start = lax.axis_index("section") == 0
    at_end = lax.axis_index("section") == lax.axis_size("section") - 1
    for replica, flag, ref in ((0, at_start, recv_a_ref), (1, at_end, recv_b_ref)):
        for row in range(x_ref.shape[0]):
            x_ref[row] = jnp.where(flag, new_ref[replica, 0, 0, row].astype(F32), ref[row].astype(F32)).astype(BF16)

        def write(row, block):
            out_ref[replica, 0, 0, row] = block

        run_forward(lambda row: x_ref[row], params, replica, (pad_ref, taps_ref, shift_ref, act_ref, mid_ref), write,
                    channels, side)


def later_backward(channels, side, last, recv_a_ref, recv_b_ref, loss_ref, stored_ref, hid_ref, rate_ref, *refs):
    refs = list(refs)
    if last:
        part_ref, accin_ref, kernel_ref, bias_ref, mixing_ref, grads_ref, send_ref = refs[:7]
        refs = refs[7:]
        outs = (writer(grads_ref, (0, 0, 0)), writer(grads_ref, (1, 0, 0)))
    else:
        hid0_ref, cot_ref, accin_ref, kernel_ref, bias_ref, mixing_ref, gxa_ref, gxb_ref, part_ref, acc_ref = refs[:10]
        refs = refs[10:]
        outs = (writer(gxa_ref, ()), writer(gxb_ref, ()))
    pad_ref, slope_ref, taps_ref, back_ref, dx_ref, flat_ref, local_ref = refs[:7]
    refs = refs[7:]
    params = (kernel_ref, bias_ref, mixing_ref)
    height, width = dx_ref.shape[1:3]
    clear_margins(pad_ref, channels)
    clear_margins(slope_ref, channels)
    back_ref[:, pl.ds((back_ref.shape[1] // LANES - 1) * LANES, LANES)] = jnp.zeros((back_ref.shape[0], LANES), F32)
    at_start = lax.axis_index("section") == 0
    at_end = lax.axis_index("section") == lax.axis_size("section") - 1
    for replica, flag, ref in ((0, at_end, recv_a_ref), (1, at_start, recv_b_ref)):
        load_params(kernel_ref, bias_ref, replica, taps_ref, None, channels)
        for row in range(height):
            fill(pad_ref, row, stored_ref[replica, 0, 0, 0, row].astype(F32), channels)

        def read(row):
            return jnp.where(flag, loss_ref[replica, 0, 0, row].astype(F32), ref[row].astype(F32)).astype(BF16)

        run_backward(read, params, replica, (pad_ref, slope_ref), taps_ref, (back_ref, dx_ref, flat_ref),
                     rate_ref, (replica,), outs[replica], local_ref, channels, side)
        mixed = mix_grad(hid_ref[replica], flat_ref[...])
        if last:
            rows_ref, turn_ref, stage_ref = refs
            pack_grads(channels, side * side + 1, replica, mixed, part_ref, local_ref, accin_ref, rows_ref, turn_ref, stage_ref, send_ref)
        else:
            for row in range(height):
                flat_ref[pl.ds(row * width, width), :] = cot_ref[replica, 0, 0, row]
            part_ref[replica] = mixed + mix_grad(hid0_ref[replica], flat_ref[...])
            acc_ref[replica] = accin_ref[replica] + local_ref[...]


def pack_grads(channels, used, replica, mixed, part_ref, local_ref, accin_ref, rows_ref, turn_ref, stage_ref, send_ref):
    tiles = tiles_of(channels)
    shards, both, _ = send_ref.shape
    share = both // 2
    edge = span_of(tiles - 1, channels)
    total = mixed + part_ref[replica]
    for tile in range(tiles):
        span = span_of(tile, channels)
        rows_ref[tile, :, 0:span] = total[:, tile * LANES : tile * LANES + span]
    for tile in range(tiles):
        span = span_of(tile, channels)
        count = used
        turn_ref[...] = jnp.zeros(turn_ref.shape, F32)
        turn_ref[pl.ds(edge, count), :] = local_ref[tile, 0:count] + accin_ref[replica, tile, 0:count]
        turned = jnp.transpose(turn_ref[...])
        rows_ref[tiles - 1, pl.ds(tile * LANES, span), edge:LANES] = turned[0:span, edge:LANES]
    for shard in range(shards):
        for tile in range(tiles):
            stage_ref[shard, tile, pl.ds(replica * share, share), :] = rows_ref[tile, pl.ds(shard * share, share), :]
    if replica == 1:
        for shard in range(shards):
            for tile in range(tiles):
                send_ref[shard, :, pl.ds(tile * LANES, LANES)] = stage_ref[shard, tile].astype(BF16)


def sum_shares(recv_ref, own_ref, cross_ref):
    shards, both, _ = recv_ref.shape
    share = both // 2
    total = recv_ref[0].astype(F32)
    for shard in range(1, shards):
        total = total + recv_ref[shard].astype(F32)
    own_ref[...] = total[0:share]
    cross_ref[...] = total[share:both].astype(BF16)


def finish(channels, side, factor, own_ref, cross_ref, kernel_ref, bias_ref, mixing_ref, turn_ref):
    share = own_ref.shape[0]
    edge = channels % LANES
    base = (tiles_of(channels) - 1) * LANES
    total = (own_ref[...] + cross_ref[...].astype(F32)) * factor
    mixing_ref[0, 0] = total[:, 0:channels]
    turn_ref[...] = jnp.zeros(turn_ref.shape, F32)
    turn_ref[0:share, :] = total[:, base : base + LANES]
    turned = jnp.transpose(turn_ref[...])
    for tap_row in range(side):
        kernel_ref[0, 0, tap_row] = turned[edge + tap_row * side : edge + (tap_row + 1) * side, 0:share]
    bias_ref[0] = turned[edge + side * side : edge + side * side + 1, 0:share]


def whole(array):
    return pl.BlockSpec(array.shape, lambda step: (0,) * len(array.shape))


def tick_of(array, tick):
    shape = (array.shape[0], 1) + array.shape[2:]
    return pl.BlockSpec(shape, lambda step: (0, tick) + (0,) * (len(shape) - 2))


def call(body, args, outs, scratch, name):
    specs = [whole(a) if not isinstance(a, tuple) else tick_of(*a) for a in args]
    args = [a if not isinstance(a, tuple) else a[0] for a in args]
    return pl.pallas_call(
        body,
        out_shape=outs,
        grid=(1,),
        in_specs=specs,
        out_specs=jax.tree.map(whole, outs),
        scratch_shapes=scratch,
        name=name,
        compiler_params=pltpu.CompilerParams(vmem_limit_bytes=40 * 1024 * 1024),
    )(*args)


def move(block, distance):
    count = lax.axis_size("section")
    route = [(i - distance, i) for i in range(count) if 0 <= i - distance < count]
    return lax.ppermute(block, "section", route)


def per_device(activations, stored_inputs, cotangents, new_inputs, loss_grad, depth_kernel, depth_bias, mixing):
    sections = lax.axis_size("section")
    shards = lax.axis_size("dp")
    height, width, channels = activations.shape[3:]
    side = depth_kernel.shape[3]
    tick_count = stored_inputs.shape[1]
    tiles = tiles_of(channels)
    wide = tiles * LANES
    spots = height * width
    params = (depth_kernel, depth_bias, mixing)
    struct = jax.ShapeDtypeStruct
    maps = struct((height, width, channels), BF16)
    hids = struct((2, spots, channels), BF16)
    rates = struct((2, tiles, height, width, LANES), F32)
    accs = struct((2, tiles, 32, LANES), F32)
    parts = struct((2, channels, channels), F32)
    pad = pltpu.VMEM((tiles, height, width + 2 * SUB, LANES), F32)
    taps = pltpu.VMEM((tiles, 32, LANES), F32)
    shift = pltpu.VMEM((tiles, SUB, LANES), F32)
    act = pltpu.VMEM((tiles, height, width, LANES), F32)
    back = pltpu.VMEM((spots, wide), F32)
    flat = pltpu.VMEM((spots, channels), BF16)
    local = pltpu.VMEM((tiles, 32, LANES), F32)
    bind = functools.partial

    gxa, gxb, hid0, acc = call(
        bind(first_backward, channels, side), ((stored_inputs, 0), cotangents) + params,
        (maps, maps, hids, accs), [pad, pad, taps, shift, act, act, back, act, flat], "back0")
    ga = move(gxa, -1)
    gb = move(gxb, 1)
    fscratch = [pad, taps, shift, act, flat, pltpu.VMEM((height, width, channels), BF16)]
    fa, fb, hid1, rate = call(
        bind(forward_recompute, channels, side, False), (activations, (stored_inputs, 1)) + params,
        (maps, maps, hids, rates), fscratch, "fwd0")
    xa = move(fa, 1)
    xb = move(fb, -1)
    bscratch = [pad, pad, taps, back, act, flat, local]
    gxa, gxb, part, acc = call(
        bind(later_backward, channels, side, False),
        (ga, gb, (loss_grad, 0), (stored_inputs, 1), hid1, rate, hid0, cotangents, acc) + params,
        (maps, maps, parts, accs), bscratch, "back1")
    ga = move(gxa, -1)
    gb = move(gxb, 1)
    fa, fb, hid2, rate = call(
        bind(forward_recompute, channels, side, True), (xa, xb, (new_inputs, 0), (stored_inputs, 2)) + params,
        (maps, maps, hids, rates), fscratch, "fwd1")
    xa = move(fa, 1)
    xb = move(fb, -1)
    share = channels // shards
    both = struct((shards, 2 * share, wide), BF16)
    pair = struct((2, 1, 1, height, width, channels), BF16)
    input_grads, send = call(
        bind(later_backward, channels, side, True),
        (ga, gb, (loss_grad, 1), (stored_inputs, 2), hid2, rate, part, acc) + params,
        (pair, both),
        bscratch + [pltpu.VMEM((tiles, channels, LANES), F32), pltpu.VMEM((LANES, LANES), F32),
                    pltpu.VMEM((shards, tiles, 2 * share, LANES), F32)], "back2")
    spread_out = lax.all_to_all(send, "dp", split_axis=0, concat_axis=0, tiled=True)
    section_outputs = call(
        bind(last_forward, channels, side), (xa, xb, (new_inputs, 1)) + params, pair, fscratch, "fwd2")
    own, cross = call(
        sum_shares, (spread_out,), (struct((share, wide), F32), struct((share, wide), BF16)), [], "shares")
    cross = lax.ppermute(cross, "section", [(i, sections - 1 - i) for i in range(sections)])
    factor = float((2.0 * tick_count * shards * spots) ** (-0.5))
    grad_kernel, grad_bias, grad_mixing = call(
        bind(finish, channels, side, factor), (own, cross),
        (struct((1, 1, side, side, share), F32), struct((1, 1, share), F32), struct((1, 1, share, channels), F32)),
        [pltpu.VMEM((LANES, LANES), F32)], "finish")
    return (section_outputs, input_grads, grad_kernel, grad_bias, grad_mixing)


def solution(mesh):
    return jax.shard_map(
        per_device,
        mesh=mesh,
        in_specs=(
            P(None, "section", "dp", None, None, None),
            P(None, None, "section", "dp", None, None, None),
            P(None, "section", "dp", None, None, None),
            P(None, None, "dp", None, None, None),
            P(None, None, "dp", None, None, None),
            P("section", None, None, None, None, None),
            P("section", None, None, None),
            P("section", None, None, None, None),
        ),
        out_specs=(
            P(None, "section", "dp", None, None, None),
            P(None, "section", "dp", None, None, None),
            P("section", None, None, None, "dp"),
            P("section", None, "dp"),
            P("section", None, "dp", None),
        ),
        check_vma=False,
    )
```

profile of v0, /device:TPU:8, one launch (start us, length us, event | category | flops | bytes accessed | tf_op | source)
XLA Modules:
  0.0 98.1 jit_solution(9234883721127756597)
XLA Ops:
  0.6 0.8 copy.13.refs_2_.refs_4_.kernel_ref.refs_3_
  1.5 0.0 copy-start
  1.5 1.4 %copy-done = bf16[2,3,1,1,8,32,416]{6,5,4,3,2,1,0:T(8,128)(2,1)S(1)} copy-done((bf16[2,3,1,1,8,32,416]{6,5,4,3,2,1,0:T(8,128)(2,1)S(1)}, bf16[2,3,1,1,8,32,416]{6,5,4,3,2,1,0:T(8,128)(2,1)}, u32[]{:S(2)}) %copy-start) | copy-done | bytes 1277976
  2.9 0.0 copy-start.2
  2.9 1.2 %copy-done.2 = bf16[1,2,1,416,416]{4,3,2,1,0:T(8,128)(2,1)S(1)} copy-done((bf16[1,2,1,416,416]{4,3,2,1,0:T(8,128)(2,1)S(1)}, bf16[1,2,1,416,416]{4,3,2,1,0:T(8,128)(2,1)}, u32[]{:S(2)}) %copy-start.2) | copy-done | bytes 692248
  4.0 0.0 copy-start.6
  4.0 1.0 %copy-done.6 = bf16[2,1,1,8,32,416]{5,4,3,2,1,0:T(8,128)(2,1)S(1)} copy-done((bf16[2,1,1,8,32,416]{5,4,3,2,1,0:T(8,128)(2,1)S(1)}, bf16[2,1,1,8,32,416]{5,4,3,2,1,0:T(8,128)(2,1)}, u32[]{:S(2)}) %copy-start.6) | copy-done | bytes 426008
  5.1 0.0 copy-start.10
  5.1 0.7 copy-done.10
  5.8 0.0 copy-start.1
  5.8 0.0 copy-start.3
  5.8 0.0 copy-start.9
  5.8 6.4 %back0.1 = (bf16[8,32,416]{2,1,0:T(8,128)(2,1)S(1)}, bf16[8,32,416]{2,1,0:T(8,128)(2,1)S(1)}, bf16[2,256,416]{2,1,0:T(8,128)(2,1)S(1)}, f32[2,4,32,128]{3,2,1,0:T(8,128)S(1)}) custom-call(bf16[2,3,1,1,8,32,416]{6,5,4,3,2,1,0:T(8,128)(2,1)S(1)} %copy-done, bf16[2,1,1,8,32,416]{5,4,3,2,1,0:T(8,128)(2,1)S(1)} %copy-done.6, ...), custom_call_target="tpu_custom_call" | custom-call | tf_op jit(solution)/shard_map/back0/pallas_call | solution.py:395
  12.1 0.0 copy-start.5
  12.2 0.0 copy-start.7
  12.2 0.0 copy-start.11
  12.2 6.0 %collective-permute-start.4 = (bf16[8,32,416]{2,1,0:T(8,128)(2,1)S(1)}, bf16[8,32,416]{2,1,0:T(8,128)(2,1)S(1)}, u32[]{:S(2)}, u32[]{:S(2)}) collective-permute-start(bf16[8,32,416]{2,1,0:T(8,128)(2,1)S(1)} %get-tuple-element.32), channel_id=1, source_target_pairs={{8,0},{16,8},{24,16},{32,24},{40,32},{48,40},{56,48},{64,56},{72,6... | collective-permute-start | bytes 638984 | tf_op jit(solution)/shard_map/ppermute | solution.py:410
  18.2 1.9 %collective-permute-start.5 = (bf16[8,32,416]{2,1,0:T(8,128)(2,1)S(1)}, bf16[8,32,416]{2,1,0:T(8,128)(2,1)S(1)}, u32[]{:S(2)}, u32[]{:S(2)}) collective-permute-start(bf16[8,32,416]{2,1,0:T(8,128)(2,1)S(1)} %get-tuple-element.33), channel_id=1, source_target_pairs={{0,8},{8,16},{16,24},{24,32},{32,40},{40,48},{48,56},{56,64},{64,7... | collective-permute-start | bytes 638984 | tf_op jit(solution)/shard_map/ppermute | solution.py:410
  20.1 0.0 copy-done.1
  20.1 0.0 copy-done.3
  20.1 0.0 copy-done.9
  20.1 4.7 %fwd0.1 = (bf16[8,32,416]{2,1,0:T(8,128)(2,1)S(1)}, bf16[8,32,416]{2,1,0:T(8,128)(2,1)S(1)}, bf16[2,256,416]{2,1,0:T(8,128)(2,1)S(1)}, f32[2,4,8,32,128]{4,3,2,1,0:T(8,128)S(1)}) custom-call(bf16[2,1,1,8,32,416]{5,4,3,2,1,0:T(8,128)(2,1)S(1)} %copy-done.9, bf16[2,3,1,1,8,32,416]{6,5,4,3,2,1,0:T(8,128)(2,1)S(1)} %copy-done.1, ...), custom_call_target="tpu_custom_call" | custom-call | tf_op jit(solution)/shard_map/fwd0/pallas_call | solution.py:395
  24.9 1.9 %collective-permute-start = (bf16[8,32,416]{2,1,0:T(8,128)(2,1)S(1)}, bf16[8,32,416]{2,1,0:T(8,128)(2,1)S(1)}, u32[]{:S(2)}, u32[]{:S(2)}) collective-permute-start(bf16[8,32,416]{2,1,0:T(8,128)(2,1)S(1)} %get-tuple-element.28), channel_id=1, source_target_pairs={{0,8},{8,16},{16,24},{24,32},{32,40},{40,48},{48,56},{56,64},{64,7... | collective-permute-start | bytes 638984 | tf_op jit(solution)/shard_map/ppermute | solution.py:410
  26.8 6.3 %collective-permute-start.1 = (bf16[8,32,416]{2,1,0:T(8,128)(2,1)S(1)}, bf16[8,32,416]{2,1,0:T(8,128)(2,1)S(1)}, u32[]{:S(2)}, u32[]{:S(2)}) collective-permute-start(bf16[8,32,416]{2,1,0:T(8,128)(2,1)S(1)} %get-tuple-element.29), channel_id=1, source_target_pairs={{8,0},{16,8},{24,16},{32,24},{40,32},{48,40},{56,48},{64,56},{72,6... | collective-permute-start | bytes 638984 | tf_op jit(solution)/shard_map/ppermute | solution.py:410
  33.1 0.0 collective-permute-done.4.recv_a_ref
  33.2 0.0 collective-permute-done.5.recv_b_ref
  33.2 0.0 copy-done.5
  33.2 0.0 copy-done.7
  33.2 0.0 copy-done.11
  33.2 0.0 copy-start.4
  33.2 4.9 %back1.1 = (bf16[8,32,416]{2,1,0:T(8,128)(2,1)S(1)}, bf16[8,32,416]{2,1,0:T(8,128)(2,1)S(1)}, f32[2,416,416]{2,1,0:T(8,128)S(1)}, f32[2,4,32,128]{3,2,1,0:T(8,128)S(1)}) custom-call(bf16[8,32,416]{2,1,0:T(8,128)(2,1)S(1)} %collective-permute-done.4.recv_a_ref, bf16[8,32,416]{2,1,0:T(8,128)(2,1)S(1)} %collective-permute-done.5.recv_b_ref, ...), custom_call_target="tpu_custom_call" | custom-call | tf_op jit(solution)/shard_map/back1/pallas_call | solution.py:395
  38.1 2.4 %collective-permute-start.6 = (bf16[8,32,416]{2,1,0:T(8,128)(2,1)S(1)}, bf16[8,32,416]{2,1,0:T(8,128)(2,1)S(1)}, u32[]{:S(2)}, u32[]{:S(2)}) collective-permute-start(bf16[8,32,416]{2,1,0:T(8,128)(2,1)S(1)} %get-tuple-element.38), channel_id=1, source_target_pairs={{8,0},{16,8},{24,16},{32,24},{40,32},{48,40},{56,48},{64,56},{72,6... | collective-permute-start | bytes 638984 | tf_op jit(solution)/shard_map/ppermute | solution.py:410
  40.5 1.9 %collective-permute-start.7 = (bf16[8,32,416]{2,1,0:T(8,128)(2,1)S(1)}, bf16[8,32,416]{2,1,0:T(8,128)(2,1)S(1)}, u32[]{:S(2)}, u32[]{:S(2)}) collective-permute-start(bf16[8,32,416]{2,1,0:T(8,128)(2,1)S(1)} %get-tuple-element.39), channel_id=1, source_target_pairs={{0,8},{8,16},{16,24},{24,32},{32,40},{40,48},{48,56},{56,64},{64,7... | collective-permute-start | bytes 638984 | tf_op jit(solution)/shard_map/ppermute | solution.py:410
  42.4 0.0 collective-permute-done.refs_0_
  42.4 0.0 collective-permute-done.1.refs_1_
  42.4 0.0 copy-done.4
  42.4 5.3 %fwd1.1 = (bf16[8,32,416]{2,1,0:T(8,128)(2,1)}, bf16[8,32,416]{2,1,0:T(8,128)(2,1)S(1)}, bf16[2,256,416]{2,1,0:T(8,128)(2,1)S(1)}, f32[2,4,8,32,128]{4,3,2,1,0:T(8,128)S(1)}) custom-call(bf16[8,32,416]{2,1,0:T(8,128)(2,1)S(1)} %collective-permute-done.refs_0_, bf16[8,32,416]{2,1,0:T(8,128)(2,1)S(1)} %collective-permute-done.1.refs_1_, ...), custom_call_target="tpu_custom_call" | custom-call | tf_op jit(solution)/shard_map/fwd1/pallas_call | solution.py:395
  47.7 0.0 copy-start.13
  47.7 0.7 copy-done.13
  48.4 0.0 collective-permute-done.6.recv_a_ref
  48.4 2.4 %collective-permute-done.7.recv_b_ref = bf16[8,32,416]{2,1,0:T(8,128)(2,1)S(1)} collective-permute-done((bf16[8,32,416]{2,1,0:T(8,128)(2,1)S(1)}, bf16[8,32,416]{2,1,0:T(8,128)(2,1)S(1)}, u32[]{:S(2)}, u32[]{:S(2)}) %collective-permute-start.7) | collective-permute-done | bytes 213024 | tf_op jit(solution)/shard_map/ppermute | solution.py:410
  50.9 5.6 %back2.1 = (bf16[2,1,1,8,32,416]{5,4,3,2,1,0:T(8,128)(2,1)}, bf16[8,104,512]{2,1,0:T(8,128)(2,1)S(1)}) custom-call(bf16[8,32,416]{2,1,0:T(8,128)(2,1)S(1)} %collective-permute-done.6.recv_a_ref, bf16[8,32,416]{2,1,0:T(8,128)(2,1)S(1)} %collective-permute-done.7.recv_b_ref, bf16[2,2,1,8,32,416]{5,4,3,2,1,0:T(8,128)(2,1)S(1)} %copy-done.5, ...), custom_call_target="tpu_custom_call" | custom-call | tf_op jit(solution)/shard_map/back2/pallas_call | solution.py:395
  56.5 0.0 copy-start.8
  56.5 0.9 copy-done.8
  57.4 0.0 copy-start.12
  57.4 8.4 %all-to-all-start = ((bf16[8,104,512]{2,1,0:T(8,128)(2,1)}), bf16[8,104,512]{2,1,0:T(8,128)(2,1)S(1)}, u32[]{:S(2)}, u32[]{:S(2)}) async-start(bf16[8,104,512]{2,1,0:T(8,128)(2,1)} %copy-done.8), calls=%async_computation | async-start | bytes 1703936 | tf_op jit(solution)/shard_map/all_to_all | solution.py:470
  65.7 1.9 %collective-permute-start.2 = (bf16[8,32,416]{2,1,0:T(8,128)(2,1)}, bf16[8,32,416]{2,1,0:T(8,128)(2,1)S(1)}, u32[]{:S(2)}, u32[]{:S(2)}) collective-permute-start(bf16[8,32,416]{2,1,0:T(8,128)(2,1)} %get-tuple-element.30), channel_id=1, source_target_pairs={{0,8},{8,16},{16,24},{24,32},{32,40},{40,48},{48,56},{56,64},{64,7... | collective-permute-start | bytes 638984 | tf_op jit(solution)/shard_map/ppermute | solution.py:410
  67.7 6.3 %collective-permute-start.3 = (bf16[8,32,416]{2,1,0:T(8,128)(2,1)}, bf16[8,32,416]{2,1,0:T(8,128)(2,1)S(1)}, u32[]{:S(2)}, u32[]{:S(2)}) collective-permute-start(bf16[8,32,416]{2,1,0:T(8,128)(2,1)} %copy-done.13), channel_id=1, source_target_pairs={{8,0},{16,8},{24,16},{32,24},{40,32},{48,40},{56,48},{64,56},{72,6... | collective-permute-start | bytes 638984 | tf_op jit(solution)/shard_map/ppermute | solution.py:410
  74.0 15.6 %all-to-all-done.recv_ref = bf16[8,104,512]{2,1,0:T(8,128)(2,1)S(1)} async-done(((bf16[8,104,512]{2,1,0:T(8,128)(2,1)}), bf16[8,104,512]{2,1,0:T(8,128)(2,1)S(1)}, u32[]{:S(2)}, u32[]{:S(2)}) %all-to-all-start) | async-done | bytes 852000 | tf_op jit(solution)/shard_map/all_to_all | solution.py:470
  89.6 0.1 shares.1
  89.8 0.1 collective-permute-start.8
  89.9 0.0 collective-permute-done.2.recv_a_ref
  89.9 0.0 collective-permute-done.3.recv_b_ref
  89.9 0.0 copy-done.12
  89.9 3.4 %fwd2.1 = bf16[2,1,1,8,32,416]{5,4,3,2,1,0:T(8,128)(2,1)} custom-call(bf16[8,32,416]{2,1,0:T(8,128)(2,1)S(1)} %collective-permute-done.2.recv_a_ref, bf16[8,32,416]{2,1,0:T(8,128)(2,1)S(1)} %collective-permute-done.3.recv_b_ref, bf16[2,2,1,8,32,416]{5,4,3,2,1,0:T(8,128)(2,1)S(1)} %copy-done.4, ...), custom_call_target="tpu_custom_call" | custom-call | tf_op jit(solution)/shard_map/fwd2/pallas_call | solution.py:395
  93.3 2.8 %collective-permute-done.8.cross_ref = bf16[52,512]{1,0:T(8,128)(2,1)S(1)} collective-permute-done((bf16[52,512]{1,0:T(8,128)(2,1)S(1)}, bf16[52,512]{1,0:T(8,128)(2,1)S(1)}, u32[]{:S(2)}, u32[]{:S(2)}) %collective-permute-start.8) | collective-permute-done | bytes 53280 | tf_op jit(solution)/shard_map/ppermute | solution.py:475
  96.2 0.6 finish.1
  96.8 0.6 copy.19
  97.4 0.8 copy.20
Async XLA Ops:
  1.5 1.4 %copy-start = (bf16[2,3,1,1,8,32,416]{6,5,4,3,2,1,0:T(8,128)(2,1)S(1)}, bf16[2,3,1,1,8,32,416]{6,5,4,3,2,1,0:T(8,128)(2,1)}, u32[]{:S(2)}) copy-start(bf16[2,3,1,1,8,32,416]{6,5,4,3,2,1,0:T(8,128)(2,1)} %stored_ref.5) | copy-start | bytes 3833860
  2.9 1.2 %copy-start.2 = (bf16[1,2,1,416,416]{4,3,2,1,0:T(8,128)(2,1)S(1)}, bf16[1,2,1,416,416]{4,3,2,1,0:T(8,128)(2,1)}, u32[]{:S(2)}) copy-start(bf16[1,2,1,416,416]{4,3,2,1,0:T(8,128)(2,1)} %refs_4_.6) | copy-start | bytes 2076676
  4.0 1.0 %copy-start.6 = (bf16[2,1,1,8,32,416]{5,4,3,2,1,0:T(8,128)(2,1)S(1)}, bf16[2,1,1,8,32,416]{5,4,3,2,1,0:T(8,128)(2,1)}, u32[]{:S(2)}) copy-start(bf16[2,1,1,8,32,416]{5,4,3,2,1,0:T(8,128)(2,1)} %refs_1_.3) | copy-start | bytes 1277956
  5.1 0.7 copy-start.10
  5.8 14.4 %copy-start.1 = (bf16[2,3,1,1,8,32,416]{6,5,4,3,2,1,0:T(8,128)(2,1)S(1)}, bf16[2,3,1,1,8,32,416]{6,5,4,3,2,1,0:T(8,128)(2,1)}, u32[]{:S(2)}) copy-start(bf16[2,3,1,1,8,32,416]{6,5,4,3,2,1,0:T(8,128)(2,1)} %stored_ref.5) | copy-start | bytes 3833860
  5.8 14.4 %copy-start.3 = (bf16[1,2,1,416,416]{4,3,2,1,0:T(8,128)(2,1)S(1)}, bf16[1,2,1,416,416]{4,3,2,1,0:T(8,128)(2,1)}, u32[]{:S(2)}) copy-start(bf16[1,2,1,416,416]{4,3,2,1,0:T(8,128)(2,1)} %refs_4_.6) | copy-start | bytes 2076676
  5.8 14.4 %copy-start.9 = (bf16[2,1,1,8,32,416]{5,4,3,2,1,0:T(8,128)(2,1)S(1)}, bf16[2,1,1,8,32,416]{5,4,3,2,1,0:T(8,128)(2,1)}, u32[]{:S(2)}) copy-start(bf16[2,1,1,8,32,416]{5,4,3,2,1,0:T(8,128)(2,1)} %refs_0_.1) | copy-start | bytes 1277956
  12.1 21.0 %copy-start.5 = (bf16[2,2,1,8,32,416]{5,4,3,2,1,0:T(8,128)(2,1)S(1)}, bf16[2,2,1,8,32,416]{5,4,3,2,1,0:T(8,128)(2,1)}, u32[]{:S(2)}) copy-start(bf16[2,2,1,8,32,416]{5,4,3,2,1,0:T(8,128)(2,1)} %loss_ref.3) | copy-start | bytes 2555908
  12.2 21.0 %copy-start.7 = (bf16[2,1,1,8,32,416]{5,4,3,2,1,0:T(8,128)(2,1)S(1)}, bf16[2,1,1,8,32,416]{5,4,3,2,1,0:T(8,128)(2,1)}, u32[]{:S(2)}) copy-start(bf16[2,1,1,8,32,416]{5,4,3,2,1,0:T(8,128)(2,1)} %refs_1_.3) | copy-start | bytes 1277956
  12.2 21.0 %copy-start.11 = (f32[1,2,1,416]{3,2,1,0:T(1,128)S(1)}, f32[1,2,1,416]{3,2,1,0:T(1,128)}, u32[]{:S(2)}) copy-start(f32[1,2,1,416]{3,2,1,0:T(1,128)} %refs_3_.6) | copy-start | bytes 9988
  12.2 21.0 %collective-permute-start.4 = (bf16[8,32,416]{2,1,0:T(8,128)(2,1)S(1)}, bf16[8,32,416]{2,1,0:T(8,128)(2,1)S(1)}, u32[]{:S(2)}, u32[]{:S(2)}) collective-permute-start(bf16[8,32,416]{2,1,0:T(8,128)(2,1)S(1)} %get-tuple-element.32), channel_id=1, source_target_pairs={{8,0},{16,8},{24,16},{32,24},{40,32},{48,40},{56,48},{64,56},{72,6... | collective-permute-start | bytes 638984 | tf_op jit(solution)/shard_map/ppermute | solution.py:410
  18.2 15.0 %collective-permute-start.5 = (bf16[8,32,416]{2,1,0:T(8,128)(2,1)S(1)}, bf16[8,32,416]{2,1,0:T(8,128)(2,1)S(1)}, u32[]{:S(2)}, u32[]{:S(2)}) collective-permute-start(bf16[8,32,416]{2,1,0:T(8,128)(2,1)S(1)} %get-tuple-element.33), channel_id=1, source_target_pairs={{0,8},{8,16},{16,24},{24,32},{32,40},{40,48},{48,56},{56,64},{64,7... | collective-permute-start | bytes 638984 | tf_op jit(solution)/shard_map/ppermute | solution.py:410
  24.9 17.5 %collective-permute-start = (bf16[8,32,416]{2,1,0:T(8,128)(2,1)S(1)}, bf16[8,32,416]{2,1,0:T(8,128)(2,1)S(1)}, u32[]{:S(2)}, u32[]{:S(2)}) collective-permute-start(bf16[8,32,416]{2,1,0:T(8,128)(2,1)S(1)} %get-tuple-element.28), channel_id=1, source_target_pairs={{0,8},{8,16},{16,24},{24,32},{32,40},{40,48},{48,56},{56,64},{64,7... | collective-permute-start | bytes 638984 | tf_op jit(solution)/shard_map/ppermute | solution.py:410
  26.8 15.6 %collective-permute-start.1 = (bf16[8,32,416]{2,1,0:T(8,128)(2,1)S(1)}, bf16[8,32,416]{2,1,0:T(8,128)(2,1)S(1)}, u32[]{:S(2)}, u32[]{:S(2)}) collective-permute-start(bf16[8,32,416]{2,1,0:T(8,128)(2,1)S(1)} %get-tuple-element.29), channel_id=1, source_target_pairs={{8,0},{16,8},{24,16},{32,24},{40,32},{48,40},{56,48},{64,56},{72,6... | collective-permute-start | bytes 638984 | tf_op jit(solution)/shard_map/ppermute | solution.py:410
  33.2 9.2 %copy-start.4 = (bf16[2,2,1,8,32,416]{5,4,3,2,1,0:T(8,128)(2,1)S(1)}, bf16[2,2,1,8,32,416]{5,4,3,2,1,0:T(8,128)(2,1)}, u32[]{:S(2)}) copy-start(bf16[2,2,1,8,32,416]{5,4,3,2,1,0:T(8,128)(2,1)} %new_ref.1) | copy-start | bytes 2555908
  38.1 10.4 %collective-permute-start.6 = (bf16[8,32,416]{2,1,0:T(8,128)(2,1)S(1)}, bf16[8,32,416]{2,1,0:T(8,128)(2,1)S(1)}, u32[]{:S(2)}, u32[]{:S(2)}) collective-permute-start(bf16[8,32,416]{2,1,0:T(8,128)(2,1)S(1)} %get-tuple-element.38), channel_id=1, source_target_pairs={{8,0},{16,8},{24,16},{32,24},{40,32},{48,40},{56,48},{64,56},{72,6... | collective-permute-start | bytes 638984 | tf_op jit(solution)/shard_map/ppermute | solution.py:410
  40.5 10.4 %collective-permute-start.7 = (bf16[8,32,416]{2,1,0:T(8,128)(2,1)S(1)}, bf16[8,32,416]{2,1,0:T(8,128)(2,1)S(1)}, u32[]{:S(2)}, u32[]{:S(2)}) collective-permute-start(bf16[8,32,416]{2,1,0:T(8,128)(2,1)S(1)} %get-tuple-element.39), channel_id=1, source_target_pairs={{0,8},{8,16},{16,24},{24,32},{32,40},{40,48},{48,56},{56,64},{64,7... | collective-permute-start | bytes 638984 | tf_op jit(solution)/shard_map/ppermute | solution.py:410
  47.7 0.7 copy-start.13
  56.5 0.9 copy-start.8
  57.4 32.5 %copy-start.12 = (f32[1,2,1,416]{3,2,1,0:T(1,128)S(1)}, f32[1,2,1,416]{3,2,1,0:T(1,128)}, u32[]{:S(2)}) copy-start(f32[1,2,1,416]{3,2,1,0:T(1,128)} %refs_3_.6) | copy-start | bytes 9988
  57.4 32.3 %all-to-all-start = ((bf16[8,104,512]{2,1,0:T(8,128)(2,1)}), bf16[8,104,512]{2,1,0:T(8,128)(2,1)S(1)}, u32[]{:S(2)}, u32[]{:S(2)}) async-start(bf16[8,104,512]{2,1,0:T(8,128)(2,1)} %copy-done.8), calls=%async_computation | async-start | bytes 1703936 | tf_op jit(solution)/shard_map/all_to_all | solution.py:470
  65.7 24.1 %collective-permute-start.2 = (bf16[8,32,416]{2,1,0:T(8,128)(2,1)}, bf16[8,32,416]{2,1,0:T(8,128)(2,1)S(1)}, u32[]{:S(2)}, u32[]{:S(2)}) collective-permute-start(bf16[8,32,416]{2,1,0:T(8,128)(2,1)} %get-tuple-element.30), channel_id=1, source_target_pairs={{0,8},{8,16},{16,24},{24,32},{32,40},{40,48},{48,56},{56,64},{64,7... | collective-permute-start | bytes 638984 | tf_op jit(solution)/shard_map/ppermute | solution.py:410
  67.7 22.2 %collective-permute-start.3 = (bf16[8,32,416]{2,1,0:T(8,128)(2,1)}, bf16[8,32,416]{2,1,0:T(8,128)(2,1)S(1)}, u32[]{:S(2)}, u32[]{:S(2)}) collective-permute-start(bf16[8,32,416]{2,1,0:T(8,128)(2,1)} %copy-done.13), channel_id=1, source_target_pairs={{8,0},{16,8},{24,16},{32,24},{40,32},{48,40},{56,48},{64,56},{72,6... | collective-permute-start | bytes 638984 | tf_op jit(solution)/shard_map/ppermute | solution.py:410
  89.8 6.4 %collective-permute-start.8 = (bf16[52,512]{1,0:T(8,128)(2,1)S(1)}, bf16[52,512]{1,0:T(8,128)(2,1)S(1)}, u32[]{:S(2)}, u32[]{:S(2)}) collective-permute-start(bf16[52,512]{1,0:T(8,128)(2,1)S(1)} %get-tuple-element.47), channel_id=1, source_target_pairs={{0,248},{8,240},{16,232},{24,224},{32,216},{40,208},{48,200},{56,1... | collective-permute-start | bytes 159752 | tf_op jit(solution)/shard_map/ppermute | solution.py:475
where the time goes:
time: 98.7 us; the launch traced here: 98.1 us
  starting transfers between devices  37.2 us (38%)
  Pallas kernels  30.9 us (31%)
  waiting for transfers between devices  20.9 us (21%)
  local copies, waits for them, and re-layouts  8.15 us (8%)
    pallas_call x8, Pallas kernels, call(): pl.pallas_call(body, out_shape=outs, grid=(1,), in_specs=specs, out_specs...  30.9 us
    ppermute x8, starting transfers between devices, move(): return lax.ppermute(block, 'section', route)  28.7 us
    all_to_all x1, waiting for transfers between devices, per_device(): lax.all_to_all(send, 'dp', split_axis=0, concat_axis=0, tiled=True)  15.6 us
    all_to_all x1, starting transfers between devices, per_device(): lax.all_to_all(send, 'dp', split_axis=0, concat_axis=0, tiled=True)  8.35 us
    unnamed x31, local copies, waits for them, and re-layouts  8.15 us
    ppermute x1, waiting for transfers between devices, per_device(): lax.ppermute(cross, 'section', [(i, sections - 1 - i) for i in range(sect...  2.85 us
    ppermute x8, waiting for transfers between devices, move(): return lax.ppermute(block, 'section', route)  2.45 us
  transfers between devices with their start and end apart: 10, of which 3 were waited for; matrix products, arithmetic and copies ran while one was open for 0% of the time, Pallas kernels for 19%

commit v1 on v0

v1 whole, which is shorter than its diff:
```python
import functools

import jax
import jax.numpy as jnp
from jax import lax
from jax.experimental import pallas as pl
from jax.experimental.pallas import tpu as pltpu
from jax.sharding import PartitionSpec as P

F32 = jnp.float32
BF16 = jnp.bfloat16
LANES = 128
SUB = 8
SLOPE = 0.7978845608028654
CUBE = 0.044715


def tiles_of(channels):
    return -(-channels // LANES)


def span_of(tile, channels):
    return min(LANES, channels - tile * LANES)


def clear_margins(pad_ref, channels):
    tiles, height, rows, _ = pad_ref.shape
    zero = jnp.zeros((SUB, LANES), F32)
    for tile in range(tiles):
        full = span_of(tile, channels) < LANES
        for row in range(height):
            starts = range(0, rows, SUB) if full else (0, rows - SUB)
            for start in starts:
                pad_ref[tile, row, pl.ds(start, SUB), :] = zero


def fill(pad_ref, row, block, channels):
    width = block.shape[0]
    for tile in range(pad_ref.shape[0]):
        span = span_of(tile, channels)
        pad_ref[tile, row, pl.ds(SUB, width), 0:span] = block[:, tile * LANES : tile * LANES + span]


def load_taps(kernel_ref, taps_ref, channels):
    tiles = taps_ref.shape[0]
    for tap in range(kernel_ref.shape[0]):
        rows = kernel_ref[tap].astype(F32)
        for tile in range(tiles):
            span = span_of(tile, channels)
            if span < LANES:
                taps_ref[tile, tap] = jnp.zeros(taps_ref.shape[2:], F32)
            taps_ref[tile, tap, :, 0:span] = rows[:, tile * LANES : tile * LANES + span]


def load_shift(bias_ref, shift_ref, channels):
    for replica in range(2):
        rows = bias_ref[0, replica]
        for tile in range(shift_ref.shape[0]):
            span = span_of(tile, channels)
            if span < LANES:
                shift_ref[tile, replica] = jnp.zeros(shift_ref.shape[2:], F32)
            shift_ref[tile, replica, 0:1, 0:span] = rows[:, tile * LANES : tile * LANES + span]


def conv_tile(pad_ref, taps_ref, replica, tile, side, flip, emit):
    margin = side // 2
    height = pad_ref.shape[1]
    width = pad_ref.shape[2] - 2 * SUB
    last = side * side - 1
    taps = [
        [
            jnp.broadcast_to(
                taps_ref[tile, last - (a * side + b) if flip else a * side + b, replica : replica + 1, :], (SUB, LANES)
            )
            for b in range(side)
        ]
        for a in range(side)
    ]
    for start in range(0, width, SUB):
        running = {}
        for source in range(height):
            window = [pad_ref[tile, source, pl.ds(SUB + start - margin + b, SUB), :] for b in range(side)]
            for a in range(side):
                row = source - (a - margin)
                if 0 <= row < height:
                    for b in range(side):
                        term = taps[a][b] * window[b]
                        running[row] = running[row] + term if row in running else term
            done = [r for r in sorted(running) if r + margin <= source or source == height - 1]
            for row in done:
                emit(row, start, running.pop(row))


def tap_grads(pad_ref, grad_ref, tile, side, acc_ref):
    margin = side // 2
    height = pad_ref.shape[1]
    width = pad_ref.shape[2] - 2 * SUB
    sums = [None] * (side * side)
    total = None
    for start in range(0, width, SUB):
        held = {}
        for source in range(height):
            window = [pad_ref[tile, source, pl.ds(SUB + start - margin + b, SUB), :] for b in range(side)]
            for a in range(side):
                row = source - (a - margin)
                if 0 <= row < height:
                    if row not in held:
                        held[row] = grad_ref[tile, row, pl.ds(SUB + start, SUB), :]
                        total = held[row] if total is None else total + held[row]
                    for b in range(side):
                        term = held[row] * window[b]
                        at = a * side + b
                        sums[at] = term if sums[at] is None else sums[at] + term
            held.pop(source - margin, None)
    for at, value in enumerate(sums + [total]):
        acc_ref[tile, pl.ds(at, 1), :] = jnp.sum(value, axis=0, keepdims=True)


def gelu_parts(u, slope):
    square = u * u
    t = jnp.tanh(u * (SLOPE + (SLOPE * CUBE) * square))
    half = 0.5 * (1.0 + t)
    hidden = u * half
    if not slope:
        return hidden, None
    rate = half + hidden * (1.0 - t) * (SLOPE + (3.0 * SLOPE * CUBE) * square)
    return hidden, rate


def activate(pad_ref, taps_ref, shift_ref, replica, side, act_ref, rate_ref, rate_at):
    def body(tile, carry):
        shift = jnp.broadcast_to(shift_ref[tile, replica, 0:1, :], (SUB, LANES))

        def emit(row, start, value):
            hidden, rate = gelu_parts(value + shift, rate_ref is not None)
            act_ref[tile, row, pl.ds(start, SUB), :] = hidden
            if rate_ref is not None:
                rate_ref[rate_at + (tile, row, pl.ds(start, SUB))] = rate

        conv_tile(pad_ref, taps_ref, replica, tile, side, False, emit)
        return carry

    lax.fori_loop(0, pad_ref.shape[0], body, 0)


def pack_hidden(act_ref, hid_ref, hid_at, channels):
    tiles, height, width, _ = act_ref.shape
    for tile in range(tiles):
        span = span_of(tile, channels)
        for row in range(height):
            hid_ref[hid_at + (pl.ds(row * width, width), pl.ds(tile * LANES, span))] = act_ref[
                tile, row, :, 0:span
            ].astype(BF16)


def run_forward(read, mixing, replica, taps_ref, shift_ref, scratch, write, channels, side):
    pad_ref, act_ref, mid_ref = scratch
    height, width = act_ref.shape[1:3]
    for row in range(height):
        fill(pad_ref, row, read(row).astype(F32), channels)
    activate(pad_ref, taps_ref, shift_ref, replica, side, act_ref, None, None)
    pack_hidden(act_ref, mid_ref, (), channels)
    mixed = jnp.dot(mid_ref[...], mixing, preferred_element_type=F32)
    for row in range(height):
        write(row, (read(row).astype(F32) + mixed[row * width : (row + 1) * width]).astype(BF16))


def run_recompute(read, replica, taps_ref, shift_ref, scratch, hid_ref, hid_at, rate_ref, rate_at, channels, side):
    pad_ref, act_ref = scratch
    for row in range(act_ref.shape[1]):
        fill(pad_ref, row, read(row).astype(F32), channels)
    activate(pad_ref, taps_ref, shift_ref, replica, side, act_ref, rate_ref, rate_at)
    pack_hidden(act_ref, hid_ref, hid_at, channels)


def run_cotangent(flat_ref, mixing, replica, taps_ref, back_ref, rate_ref, rate_at, slope_ref, dx_ref, write, channels, side):
    tiles, height, width, _ = dx_ref.shape
    back_ref[:, 0:channels] = lax.dot_general(
        flat_ref[...], mixing, (((1,), (1,)), ((), ())), preferred_element_type=F32
    )
    for tile in range(tiles):
        for row in range(height):
            slope_ref[tile, row, pl.ds(SUB, width), :] = (
                back_ref[pl.ds(row * width, width), pl.ds(tile * LANES, LANES)] * rate_ref[rate_at + (tile, row)]
            )

    def body(tile, carry):
        def emit(row, start, value):
            dx_ref[tile, row, pl.ds(start, SUB), :] = value

        conv_tile(slope_ref, taps_ref, replica, tile, side, True, emit)
        return carry

    lax.fori_loop(0, tiles, body, 0)
    for row in range(height):
        for tile in range(tiles):
            span = span_of(tile, channels)
            kept = flat_ref[pl.ds(row * width, width), pl.ds(tile * LANES, span)].astype(F32)
            write(row, tile, span, (dx_ref[tile, row, :, 0:span] + kept).astype(BF16))


def run_taps(pad_ref, slope_ref, side, acc_ref):
    def body(tile, carry):
        tap_grads(pad_ref, slope_ref, tile, side, acc_ref)
        return carry

    lax.fori_loop(0, pad_ref.shape[0], body, 0)


def clear_last(back_ref):
    rows, wide = back_ref.shape
    back_ref[:, wide - LANES : wide] = jnp.zeros((rows, LANES), F32)


def mix_grad(hid_ref, flat_ref):
    return lax.dot_general(hid_ref, flat_ref, (((0,), (0,)), ((), ())), preferred_element_type=F32)


def writer(ref, lead):
    def write(row, tile, span, block):
        ref[lead + (row, slice(None), pl.ds(tile * LANES, span))] = block

    return write


def first_kernel(channels, side, stored_hbm, cot_hbm, kernel_hbm, bias_hbm, mixing_hbm,
                 gxa_ref, gxb_ref, hid_ref, slope_ref,
                 stored_ref, cot_ref, kernel_ref, bias_ref, mixing_ref, sems,
                 pad_ref, taps_ref, shift_ref, act_ref, rate_ref, back_ref, dx_ref):
    copies = [pltpu.make_async_copy(kernel_hbm, kernel_ref, sems.at[0]),
              pltpu.make_async_copy(bias_hbm, bias_ref, sems.at[1])]
    for replica in range(2):
        copies.append(pltpu.make_async_copy(stored_hbm.at[replica, 0, 0, 0], stored_ref.at[replica], sems.at[2 + 3 * replica]))
        copies.append(pltpu.make_async_copy(mixing_hbm.at[0, replica, 0], mixing_ref.at[replica], sems.at[3 + 3 * replica]))
        copies.append(pltpu.make_async_copy(cot_hbm.at[replica, 0, 0], cot_ref.at[replica], sems.at[4 + 3 * replica]))
    for copy in copies:
        copy.start()
    height, width = act_ref.shape[1:3]
    clear_margins(pad_ref, channels)
    clear_last(back_ref)
    for replica in range(2):
        clear_margins(slope_ref.at[replica], channels)
    copies[0].wait()
    copies[1].wait()
    load_taps(kernel_ref, taps_ref, channels)
    load_shift(bias_ref, shift_ref, channels)
    for replica, out_ref in ((0, gxa_ref), (1, gxb_ref)):
        for copy in copies[2 + 3 * replica : 5 + 3 * replica]:
            copy.wait()
        run_recompute(lambda row: stored_ref[replica, row], replica, taps_ref, shift_ref, (pad_ref, act_ref),
                      hid_ref, (replica,), rate_ref, (), channels, side)
        flat_ref = cot_ref.at[replica]
        run_cotangent(flat_ref, mixing_ref[replica], replica, taps_ref, back_ref, rate_ref, (), slope_ref.at[replica],
                      dx_ref, writer(out_ref, ()), channels, side)


def entering(flag, new, old):
    return jnp.where(flag, new.astype(F32), old.astype(F32)).astype(BF16)


def ends():
    spot = lax.axis_index("section")
    return spot == 0, spot == lax.axis_size("section") - 1


def middle_kernel(channels, side, forward, *refs):
    refs = list(refs)
    if forward:
        (act_in_ref, stored_ref, next_ref, slope_ref, kernel_ref, bias_ref, mixing_ref,
         fa_ref, fb_ref, hid_ref, rate_ref, acc_ref, pad_ref, taps_ref, shift_ref, act_ref, mid_ref) = refs
    else:
        (stored_ref, next_ref, slope_ref, accin_ref, hid0_ref, cot_ref, hid1_ref, g1_ref, kernel_ref, bias_ref,
         hid_ref, rate_ref, acc_ref, part_ref, pad_ref, taps_ref, shift_ref, act_ref, local_ref) = refs
    clear_margins(pad_ref, channels)
    load_taps(kernel_ref, taps_ref, channels)
    load_shift(bias_ref, shift_ref, channels)
    for replica in range(2):
        if forward:
            out_ref = (fa_ref, fb_ref)[replica]

            def write(row, block):
                out_ref[row] = block

            run_forward(lambda row: act_in_ref[replica, 0, 0, row], mixing_ref[0, replica, 0], replica, taps_ref, shift_ref,
                        (pad_ref, act_ref, mid_ref), write, channels, side)
        run_recompute(lambda row: next_ref[replica, 0, 0, 0, row], replica, taps_ref, shift_ref, (pad_ref, act_ref),
                      hid_ref, (replica,), rate_ref, (replica,), channels, side)
        for row in range(act_ref.shape[1]):
            fill(pad_ref, row, stored_ref[replica, 0, 0, 0, row].astype(F32), channels)
        if forward:
            run_taps(pad_ref, slope_ref.at[replica], side, acc_ref.at[replica])
        else:
            run_taps(pad_ref, slope_ref.at[replica], side, local_ref)
            acc_ref[replica] = accin_ref[replica] + local_ref[...]
            part_ref[replica] = mix_grad(hid0_ref[replica], cot_ref[replica]) + mix_grad(hid1_ref[replica], g1_ref[replica])


def second_kernel(channels, side, recv_a_ref, recv_b_ref, loss_ref, rate_ref, kernel_ref, mixing_ref,
                  gxa_ref, gxb_ref, slope_ref, g1_ref, taps_ref, back_ref, dx_ref):
    height, width = dx_ref.shape[1:3]
    clear_last(back_ref)
    load_taps(kernel_ref, taps_ref, channels)
    at_start, at_end = ends()
    for replica, flag, ref, out_ref in ((0, at_end, recv_a_ref, gxa_ref), (1, at_start, recv_b_ref, gxb_ref)):
        clear_margins(slope_ref.at[replica], channels)
        for row in range(height):
            g1_ref[replica, pl.ds(row * width, width), :] = entering(flag, loss_ref[replica, 0, 0, row], ref[row])
        run_cotangent(g1_ref.at[replica], mixing_ref[0, replica, 0], replica, taps_ref, back_ref, rate_ref, (replica,),
                      slope_ref.at[replica], dx_ref, writer(out_ref, ()), channels, side)


def third_kernel(channels, side, replica, recv_ref, loss_ref, stored_ref, hid_ref, rate_ref, part_ref, accin_ref,
                 kernel_ref, mixing_ref, *refs):
    refs = list(refs)
    other_ref = refs.pop(0) if replica == 0 else None
    grads_ref, own_ref, one_ref, two_ref, three_ref = refs[:5]
    pad_ref, slope_ref, taps_ref, back_ref, dx_ref, flat_ref, local_ref, rows_ref, turn_ref, stage_ref = refs[5:]
    height, width = dx_ref.shape[1:3]
    clear_margins(pad_ref, channels)
    clear_margins(slope_ref, channels)
    clear_last(back_ref)
    load_taps(kernel_ref, taps_ref, channels)
    at_start, at_end = ends()
    flag = at_start if replica else at_end
    for row in range(height):
        flat_ref[pl.ds(row * width, width), :] = entering(flag, loss_ref[replica, 0, 0, row], recv_ref[row])
        fill(pad_ref, row, stored_ref[replica, 0, 0, 0, row].astype(F32), channels)
    if replica == 0:
        grads_ref[1, 0, 0] = other_ref[...]
        write = writer(grads_ref, (0, 0, 0))
    else:
        write = writer(grads_ref, ())
    run_cotangent(flat_ref, mixing_ref[0, replica, 0], replica, taps_ref, back_ref, rate_ref, (replica,), slope_ref, dx_ref,
                  write, channels, side)
    run_taps(pad_ref, slope_ref, side, local_ref)
    total = mix_grad(hid_ref[replica], flat_ref[...]) + part_ref[replica]
    tiles = tiles_of(channels)
    ring = stage_ref.shape[0]
    both = stage_ref.shape[2]
    share = both // 2
    edge = span_of(tiles - 1, channels)
    count = side * side + 1
    for tile in range(tiles):
        span = span_of(tile, channels)
        rows_ref[tile, :, 0:span] = total[:, tile * LANES : tile * LANES + span]
    for tile in range(tiles):
        span = span_of(tile, channels)
        turn_ref[...] = jnp.zeros(turn_ref.shape, F32)
        turn_ref[pl.ds(edge, count), :] = local_ref[tile, 0:count] + accin_ref[replica, tile, 0:count]
        turned = jnp.transpose(turn_ref[...])
        rows_ref[tiles - 1, pl.ds(tile * LANES, span), edge:LANES] = turned[0:span, edge:LANES]
    for spot in range(ring):
        for half in range(2):
            for tile in range(tiles):
                stage_ref[spot, tile, pl.ds(half * share, share), :] = rows_ref[
                    tile, pl.ds((half * ring + spot) * share, share), :
                ]
    me = lax.rem(lax.axis_index("dp"), ring)
    for tile in range(tiles):
        own_ref[:, pl.ds(tile * LANES, LANES)] = stage_ref[me, tile]
    for step, out_ref in ((1, one_ref), (2, two_ref), (3, three_ref)):
        spot = lax.rem(me + step, ring)
        for tile in range(tiles):
            out_ref[:, pl.ds(tile * LANES, LANES)] = stage_ref[spot, tile].astype(BF16)


def forward_kernel(channels, side, last, recv_a_ref, recv_b_ref, new_ref, kernel_ref, bias_ref, mixing_ref, *refs):
    outs = refs[:1] if last else refs[:2]
    pad_ref, taps_ref, shift_ref, act_ref, mid_ref, x_ref = refs[len(outs):]
    clear_margins(pad_ref, channels)
    load_taps(kernel_ref, taps_ref, channels)
    load_shift(bias_ref, shift_ref, channels)
    at_start, at_end = ends()
    for replica, flag, ref in ((0, at_start, recv_a_ref), (1, at_end, recv_b_ref)):
        for row in range(x_ref.shape[0]):
            x_ref[row] = entering(flag, new_ref[replica, 0, 0, row], ref[row])

        def write(row, block):
            if last:
                outs[0][replica, 0, 0, row] = block
            else:
                outs[replica][row] = block

        run_forward(lambda row: x_ref[row], mixing_ref[0, replica, 0], replica, taps_ref, shift_ref,
                    (pad_ref, act_ref, mid_ref), write, channels, side)


def sum_ring(own_ref, one_ref, two_ref, three_ref):
    return own_ref[...] + one_ref[...].astype(F32) + (two_ref[...].astype(F32) + three_ref[...].astype(F32))


def halves(total):
    share = total.shape[0] // 2
    low = lax.axis_index("dp") < lax.axis_size("dp") // 2
    first, second = total[0:share], total[share : 2 * share]
    return jnp.where(low, first, second), jnp.where(low, second, first)


def sum_b(own_ref, one_ref, two_ref, three_ref, near_ref, far_ref):
    near, far = halves(sum_ring(own_ref, one_ref, two_ref, three_ref))
    near_ref[...] = near.astype(BF16)
    far_ref[...] = far.astype(BF16)


def sum_a(own_ref, one_ref, two_ref, three_ref, near_ref, far_ref):
    near, far = halves(sum_ring(own_ref, one_ref, two_ref, three_ref))
    near_ref[...] = near
    far_ref[...] = far.astype(BF16)


def finish(channels, side, factor, own_ref, far_ref, cross_ref, both_ref, kernel_ref, bias_ref, mixing_ref, turn_ref):
    share = own_ref.shape[0]
    edge = channels % LANES
    base = (tiles_of(channels) - 1) * LANES
    total = own_ref[...] + far_ref[...].astype(F32) + (cross_ref[...].astype(F32) + both_ref[...].astype(F32))
    total = total * factor
    mixing_ref[:, 0, :] = total[:, 0:channels]
    turn_ref[...] = jnp.zeros(turn_ref.shape, F32)
    turn_ref[0:share, :] = total[:, base : base + LANES]
    turned = jnp.transpose(turn_ref[...])
    for tap_row in range(side):
        for tap_col in range(side):
            at = edge + tap_row * side + tap_col
            kernel_ref[tap_row, tap_col] = turned[at : at + 1, 0:share]
    bias_ref[0] = turned[edge + side * side : edge + side * side + 1, 0:share]


def whole(array):
    return pl.BlockSpec(array.shape, lambda step: (0,) * len(array.shape))


def tick_of(array, tick):
    shape = (array.shape[0], 1) + array.shape[2:]
    return pl.BlockSpec(shape, lambda step: (0, tick) + (0,) * (len(shape) - 2))


def call(body, args, outs, scratch, name, hbm=False):
    specs = [whole(a) if not isinstance(a, tuple) else tick_of(*a) for a in args]
    if hbm:
        specs = [pl.BlockSpec(memory_space=pltpu.HBM) for _ in args]
    args = [a if not isinstance(a, tuple) else a[0] for a in args]
    with jax.named_scope(name):
        return pl.pallas_call(
            body,
            out_shape=outs,
            grid=(1,),
            in_specs=specs,
            out_specs=jax.tree.map(whole, outs),
            scratch_shapes=scratch,
            name=name,
            compiler_params=pltpu.CompilerParams(vmem_limit_bytes=20 * 1024 * 1024),
        )(*args)


def move(block, distance, name):
    count = lax.axis_size("section")
    with jax.named_scope(name):
        return lax.ppermute(block, "section", [(i, (i + distance) % count) for i in range(count)])


def per_device(activations, stored_inputs, cotangents, new_inputs, loss_grad, depth_kernel, depth_bias, mixing):
    sections = lax.axis_size("section")
    shards = lax.axis_size("dp")
    ring = shards // 2
    height, width, channels = activations.shape[3:]
    side = depth_kernel.shape[3]
    tick_count = stored_inputs.shape[1]
    tiles = tiles_of(channels)
    wide = tiles * LANES
    spots = height * width
    kernels = jnp.transpose(depth_kernel, (0, 2, 3, 4, 1, 5)).reshape(side * side, 2, channels)
    struct = jax.ShapeDtypeStruct
    maps = struct((height, width, channels), BF16)
    hids = struct((2, spots, channels), BF16)
    rates = struct((2, tiles, height, width, LANES), F32)
    accs = struct((2, tiles, 32, LANES), F32)
    parts = struct((2, channels, channels), F32)
    slopes = struct((2, tiles, height, width + 2 * SUB, LANES), F32)
    pad = pltpu.VMEM((tiles, height, width + 2 * SUB, LANES), F32)
    taps = pltpu.VMEM((tiles, side * side, 2, LANES), F32)
    shift = pltpu.VMEM((tiles, 2, SUB, LANES), F32)
    act = pltpu.VMEM((tiles, height, width, LANES), F32)
    back = pltpu.VMEM((spots, wide), F32)
    flat = pltpu.VMEM((spots, channels), BF16)
    local = pltpu.VMEM((tiles, 32, LANES), F32)
    bind = functools.partial

    flat_cot = cotangents.reshape(2, 1, 1, spots, channels)
    gxa, gxb, hid0, slope = call(
        bind(first_kernel, channels, side), (stored_inputs, flat_cot, kernels, depth_bias, mixing),
        (maps, maps, hids, slopes),
        [pltpu.VMEM((2, height, width, channels), BF16), pltpu.VMEM((2, spots, channels), BF16),
         pltpu.VMEM(kernels.shape, BF16), pltpu.VMEM(depth_bias.shape, F32), pltpu.VMEM((2, channels, channels), BF16),
         pltpu.SemaphoreType.DMA((8,)), pad, taps, shift, act, act, back, act], "back0", hbm=True)
    ga = move(gxa, -1, "pc0a")
    gb = move(gxb, 1, "pc0b")
    fa, fb, hid1, rate, acc = call(
        bind(middle_kernel, channels, side, True),
        (activations, (stored_inputs, 0), (stored_inputs, 1), slope, kernels, depth_bias, mixing),
        (maps, maps, hids, rates, accs), [pad, taps, shift, act, flat], "mid0")
    xa = move(fa, 1, "pf0a")
    xb = move(fb, -1, "pf0b")
    gxa, gxb, slope, g1 = call(
        bind(second_kernel, channels, side), (ga, gb, (loss_grad, 0), rate, kernels, mixing),
        (maps, maps, slopes, hids), [taps, back, act], "back1")
    ga = move(gxa, -1, "pc1a")
    gb = move(gxb, 1, "pc1b")
    hid2, rate, acc, part = call(
        bind(middle_kernel, channels, side, False),
        ((stored_inputs, 1), (stored_inputs, 2), slope, acc, hid0, flat_cot.reshape(2, spots, channels), hid1, g1, kernels, depth_bias),
        (hids, rates, accs, parts), [pad, taps, shift, act, local], "mid1")
    share = channels // shards
    block = struct((2 * share, wide), BF16)
    held = struct((2 * share, wide), F32)
    pair = struct((2, 1, 1, height, width, channels), BF16)
    bscratch = [pad, pad, taps, back, act, flat, local,
                pltpu.VMEM((tiles, channels, LANES), F32), pltpu.VMEM((LANES, LANES), F32),
                pltpu.VMEM((ring, tiles, 2 * share, LANES), F32)]
    common = ((loss_grad, 1), (stored_inputs, 2), hid2, rate, part, acc, kernels, mixing)

    def around(blocks, name):
        got = []
        for step, item in enumerate(blocks, 1):
            route = [(i, i - i % ring + (i + step) % ring) for i in range(shards)]
            with jax.named_scope(name + str(step)):
                got.append(lax.ppermute(item, "dp", route))
        return got

    grads_b, own_b, *send_b = call(
        bind(third_kernel, channels, side, 1), (gb,) + common, (maps, held, block, block, block), bscratch, "back2b")
    got_b = around(send_b, "xb")
    input_grads, own_a, *send_a = call(
        bind(third_kernel, channels, side, 0), (ga,) + common + (grads_b,), (pair, held, block, block, block), bscratch, "back2a")
    got_a = around(send_a, "xa")
    fscratch = [pad, taps, shift, act, flat, pltpu.VMEM((height, width, channels), BF16)]
    fa, fb = call(
        bind(forward_kernel, channels, side, False), (xa, xb, (new_inputs, 0), kernels, depth_bias, mixing),
        (maps, maps), fscratch, "fwd1")
    xa = move(fa, 1, "pf1a")
    xb = move(fb, -1, "pf1b")
    quarter = struct((share, wide), BF16)
    near_b, far_b = call(sum_b, (own_b, *got_b), (quarter, quarter), [], "sumb")
    devices = [(s, d) for s in range(sections) for d in range(shards)]
    with jax.named_scope("mirror"):
        cross = lax.ppermute(near_b, "section", [(i, sections - 1 - i) for i in range(sections)])
    with jax.named_scope("mirrorz"):
        both = lax.ppermute(far_b, ("section", "dp"),
                            [(s * shards + d, (sections - 1 - s) * shards + (d + ring) % shards) for s, d in devices])
    near_a, far_a = call(sum_a, (own_a, *got_a), (struct((share, wide), F32), quarter), [], "suma")
    with jax.named_scope("across"):
        far = lax.ppermute(far_a, "dp", [(d, (d + ring) % shards) for d in range(shards)])
    section_outputs = call(
        bind(forward_kernel, channels, side, True), (xa, xb, (new_inputs, 1), kernels, depth_bias, mixing),
        pair, fscratch, "fwd2")
    factor = float((2.0 * tick_count * shards * spots) ** (-0.5))
    grad_kernel, grad_bias, grad_mixing = call(
        bind(finish, channels, side, factor), (near_a, far, cross, both),
        (struct((side, side, 1, share), F32), struct((1, 1, share), F32), struct((share, 1, channels), F32)),
        [pltpu.VMEM((LANES, LANES), F32)], "finish")
    grad_kernel = jnp.transpose(grad_kernel[None], (0, 3, 1, 2, 4))
    grad_mixing = jnp.transpose(grad_mixing[None], (0, 2, 1, 3))
    return (section_outputs, input_grads, grad_kernel, grad_bias, grad_mixing)


def solution(mesh):
    return jax.shard_map(
        per_device,
        mesh=mesh,
        in_specs=(
            P(None, "section", "dp", None, None, None),
            P(None, None, "section", "dp", None, None, None),
            P(None, "section", "dp", None, None, None),
            P(None, None, "dp", None, None, None),
            P(None, None, "dp", None, None, None),
            P("section", None, None, None, None, None),
            P("section", None, None, None),
            P("section", None, None, None, None),
        ),
        out_specs=(
            P(None, "section", "dp", None, None, None),
            P(None, "section", "dp", None, None, None),
            P("section", None, None, None, "dp"),
            P("section", None, "dp"),
            P("section", None, "dp", None),
        ),
        check_vma=False,
    )
```

time: 98.7 us -> 85.5 us (0.87)
  the two profiles are of different devices: /device:TPU:8 before, /device:TPU:6 now
where the time goes in v1:
time: 85.5 us; the launch traced here: 85.2 us
  starting transfers between devices  42.7 us (50%)
  Pallas kernels  32.6 us (38%)
  local copies, waits for them, and re-layouts  5.12 us (6%)
  waiting for transfers between devices  3.93 us (5%)
    pallas_call x11, Pallas kernels, call(): pl.pallas_call(body, out_shape=outs, grid=(1,), in_specs=specs, out_specs...  32.6 us
    ppermute x8, starting transfers between devices, move(): lax.ppermute(block, 'section', [(i, (i + distance) % count) for i in rang...  23.7 us
    ppermute x6, starting transfers between devices, around(): got.append(lax.ppermute(item, 'dp', route))  7.59 us
    ppermute x1, starting transfers between devices, per_device(): lax.ppermute(far_b, ('section', 'dp'), [(s * shards + d, (sections - 1 -...  6.87 us
    unnamed x24, local copies, waits for them, and re-layouts  5.12 us
    ppermute x1, starting transfers between devices, per_device(): lax.ppermute(far_a, 'dp', [(d, (d + ring) % shards) for d in range(shards)])  4.49 us
    ppermute x8, waiting for transfers between devices, move(): lax.ppermute(block, 'section', [(i, (i + distance) % count) for i in rang...  2.77 us
  transfers between devices with their start and end apart: 17, of which 3 were waited for; matrix products, arithmetic and copies ran while one was open for 0% of the time, Pallas kernels for 28%

profile of v1, /device:TPU:6, one launch (start us, length us, event | category | flops | bytes accessed | tf_op | source)
XLA Modules:
  0.0 85.2 jit_solution(9744840830719151983)
XLA Ops:
  0.6 0.0 copy-start
  0.6 1.4 %copy-done = bf16[2,3,1,1,8,32,416]{6,5,4,3,2,1,0:T(8,128)(2,1)S(1)} copy-done((bf16[2,3,1,1,8,32,416]{6,5,4,3,2,1,0:T(8,128)(2,1)S(1)}, bf16[2,3,1,1,8,32,416]{6,5,4,3,2,1,0:T(8,128)(2,1)}, u32[]{:S(2)}) %copy-start) | copy-done | bytes 1277976
  2.0 0.0 copy-start.2
  2.0 1.2 %copy-done.2 = bf16[1,2,1,416,416]{4,3,2,1,0:T(8,128)(2,1)S(1)} copy-done((bf16[1,2,1,416,416]{4,3,2,1,0:T(8,128)(2,1)S(1)}, bf16[1,2,1,416,416]{4,3,2,1,0:T(8,128)(2,1)}, u32[]{:S(2)}) %copy-start.2) | copy-done | bytes 692248
  3.2 0.0 copy-start.6
  3.2 0.8 copy-done.6
  4.0 0.0 copy-start.8
  4.0 1.0 %copy-done.8 = bf16[2,1,1,8,32,416]{5,4,3,2,1,0:T(8,128)(2,1)S(1)} copy-done((bf16[2,1,1,8,32,416]{5,4,3,2,1,0:T(8,128)(2,1)S(1)}, bf16[2,1,1,8,32,416]{5,4,3,2,1,0:T(8,128)(2,1)}, u32[]{:S(2)}) %copy-start.8) | copy-done | bytes 426008
  5.0 0.7 copy-done.11
  5.7 5.3 %back0.1 = (bf16[8,32,416]{2,1,0:T(8,128)(2,1)S(1)}, bf16[8,32,416]{2,1,0:T(8,128)(2,1)S(1)}, bf16[2,256,416]{2,1,0:T(8,128)(2,1)S(1)}, f32[2,4,8,48,128]{4,3,2,1,0:T(8,128)S(1)}) custom-call(bf16[2,3,1,1,8,32,416]{6,5,4,3,2,1,0:T(8,128)(2,1)S(1)} %copy-done, bf16[2,1,1,256,416]{4,3,2,1,0:T(8,128)(2,1)S(1)} %bitcast.19, bf16[25,2,416]{2,1,0:T(2,128)(2,1)S(1)} %bitcast.11, ...), custom_call_target="tpu_custom_call" | custom-call | tf_op jit(solution)/shard_map/back0/back0/pallas_call | solution.py:443
  11.1 6.6 %collective-permute-start.4 = (bf16[8,32,416]{2,1,0:T(8,128)(2,1)S(1)}, bf16[8,32,416]{2,1,0:T(8,128)(2,1)S(1)}, u32[]{:S(2)}, u32[]{:S(2)}) collective-permute-start(bf16[8,32,416]{2,1,0:T(8,128)(2,1)S(1)} %get-tuple-element.46), channel_id=1, source_target_pairs={{0,248},{8,0},{16,8},{24,16},{32,24},{40,32},{48,40},{56,48},{64,5... | collective-permute-start | bytes 638984 | tf_op jit(solution)/shard_map/pc0a/ppermute | solution.py:458
  17.7 0.0 collective-permute-start.5
  17.7 0.0 copy-done.3
  17.7 0.0 copy-done.10
  17.7 0.0 copy-start.4
  17.7 0.0 copy-start.7
  17.7 6.9 %mid0.1 = (bf16[8,32,416]{2,1,0:T(8,128)(2,1)S(1)}, bf16[8,32,416]{2,1,0:T(8,128)(2,1)S(1)}, bf16[2,256,416]{2,1,0:T(8,128)(2,1)S(1)}, f32[2,4,8,32,128]{4,3,2,1,0:T(8,128)S(1)}, f32[2,4,32,128]{3,2,1,0:T(8,128)S(1)}) custom-call(bf16[2,1,1,8,32,416]{5,4,3,2,1,0:T(8,128)(2,1)S(1)} %copy-done.10, bf16[2,3,1,1,8,32,416]{6,5,4,3,2,1,0:T(8,128)(2,1)S(1)} %copy-done, ...), custom_call_target="tpu_custom_call" | custom-call | tf_op jit(solution)/shard_map/mid0/mid0/pallas_call | solution.py:443
  24.6 0.0 collective-permute-done.4.recv_a_ref
  24.6 2.8 %collective-permute-done.5.recv_b_ref = bf16[8,32,416]{2,1,0:T(8,128)(2,1)S(1)} collective-permute-done((bf16[8,32,416]{2,1,0:T(8,128)(2,1)S(1)}, bf16[8,32,416]{2,1,0:T(8,128)(2,1)S(1)}, u32[]{:S(2)}, u32[]{:S(2)}) %collective-permute-start.5) | collective-permute-done | bytes 213024 | tf_op jit(solution)/shard_map/pc0b/ppermute | solution.py:458
  27.4 0.0 copy-done.4
  27.4 0.0 copy-done.7
  27.4 2.3 %back1.1 = (bf16[8,32,416]{2,1,0:T(8,128)(2,1)S(1)}, bf16[8,32,416]{2,1,0:T(8,128)(2,1)S(1)}, f32[2,4,8,48,128]{4,3,2,1,0:T(8,128)S(1)}, bf16[2,256,416]{2,1,0:T(8,128)(2,1)S(1)}) custom-call(bf16[8,32,416]{2,1,0:T(8,128)(2,1)S(1)} %collective-permute-done.4.recv_a_ref, bf16[8,32,416]{2,1,0:T(8,128)(2,1)S(1)} %collective-permute-done.5.recv_b_ref, ...), custom_call_target="tpu_custom_call" | custom-call | tf_op jit(solution)/shard_map/back1/back1/pallas_call | solution.py:443
  29.7 0.1 collective-permute-start.7
  29.8 5.6 %collective-permute-start.6 = (bf16[8,32,416]{2,1,0:T(8,128)(2,1)S(1)}, bf16[8,32,416]{2,1,0:T(8,128)(2,1)S(1)}, u32[]{:S(2)}, u32[]{:S(2)}) collective-permute-start(bf16[8,32,416]{2,1,0:T(8,128)(2,1)S(1)} %get-tuple-element.49), channel_id=1, source_target_pairs={{0,248},{8,0},{16,8},{24,16},{32,24},{40,32},{48,40},{56,48},{64,5... | collective-permute-start | bytes 638984 | tf_op jit(solution)/shard_map/pc1a/ppermute | solution.py:458
  35.4 0.0 collective-permute-start
  35.5 5.7 %collective-permute-start.1 = (bf16[8,32,416]{2,1,0:T(8,128)(2,1)S(1)}, bf16[8,32,416]{2,1,0:T(8,128)(2,1)S(1)}, u32[]{:S(2)}, u32[]{:S(2)}) collective-permute-start(bf16[8,32,416]{2,1,0:T(8,128)(2,1)S(1)} %get-tuple-element.43), channel_id=1, source_target_pairs={{0,248},{8,0},{16,8},{24,16},{32,24},{40,32},{48,40},{56,48},{64,5... | collective-permute-start | bytes 638984 | tf_op jit(solution)/shard_map/pf0b/ppermute | solution.py:458
  41.1 0.0 copy-done.1
  41.1 0.0 copy-done.9
  41.1 5.3 %mid1.1 = (bf16[2,256,416]{2,1,0:T(8,128)(2,1)S(1)}, f32[2,4,8,32,128]{4,3,2,1,0:T(8,128)S(1)}, f32[2,4,32,128]{3,2,1,0:T(8,128)S(1)}, f32[2,416,416]{2,1,0:T(8,128)S(1)}) custom-call(bf16[2,3,1,1,8,32,416]{6,5,4,3,2,1,0:T(8,128)(2,1)S(1)} %copy-done.1, bf16[2,3,1,1,8,32,416]{6,5,4,3,2,1,0:T(8,128)(2,1)S(1)} %copy-done.1, ...), custom_call_target="tpu_custom_call" | custom-call | tf_op jit(solution)/shard_map/mid1/mid1/pallas_call | solution.py:443
  46.4 0.0 collective-permute-done.7.recv_ref
  46.4 2.6 %back2b.1 = (bf16[8,32,416]{2,1,0:T(8,128)(2,1)S(1)}, f32[104,512]{1,0:T(8,128)S(1)}, bf16[104,512]{1,0:T(8,128)(2,1)S(1)}, bf16[104,512]{1,0:T(8,128)(2,1)S(1)}, bf16[104,512]{1,0:T(8,128)(2,1)S(1)}) custom-call(bf16[8,32,416]{2,1,0:T(8,128)(2,1)S(1)} %collective-permute-done.7.recv_ref, bf16[2,2,1,8,32,416]{5,4,3,2,1,0:T(8,128)(2,1)S(1)} %copy-done.4, ...), custom_call_target="tpu_custom_call" | custom-call | tf_op jit(solution)/shard_map/back2b/back2b/pallas_call | solution.py:443
  49.0 0.0 collective-permute-done.6.recv_ref
  49.0 0.0 copy-start.5
  49.0 3.1 %back2a.1 = (bf16[2,1,1,8,32,416]{5,4,3,2,1,0:T(8,128)(2,1)}, f32[104,512]{1,0:T(8,128)S(1)}, bf16[104,512]{1,0:T(8,128)(2,1)S(1)}, bf16[104,512]{1,0:T(8,128)(2,1)S(1)}, bf16[104,512]{1,0:T(8,128)(2,1)S(1)}) custom-call(bf16[8,32,416]{2,1,0:T(8,128)(2,1)S(1)} %collective-permute-done.6.recv_ref, bf16[2,2,1,8,32,416]{5,4,3,2,1,0:T(8,128)(2,1)S(1)} %copy-done.4, ...), custom_call_target="tpu_custom_call" | custom-call | tf_op jit(solution)/shard_map/back2a/back2a/pallas_call | solution.py:443
  52.1 0.5 collective-permute-start.8
  52.5 2.4 %collective-permute-start.9 = (bf16[104,512]{1,0:T(8,128)(2,1)S(1)}, bf16[104,512]{1,0:T(8,128)(2,1)S(1)}, u32[]{:S(2)}, u32[]{:S(2)}) collective-permute-start(bf16[104,512]{1,0:T(8,128)(2,1)S(1)} %get-tuple-element.64), channel_id=1, source_target_pairs={{0,2},{1,3},{2,0},{3,1},{4,6},{5,7},{6,4},{7,5},{8,10},{9,11},{10,... | collective-permute-start | bytes 319496 | tf_op jit(solution)/shard_map/xa2/ppermute | solution.py:526
  55.0 0.0 collective-permute-start.10
  55.0 0.0 collective-permute-done.recv_a_ref
  55.0 0.0 collective-permute-done.1.recv_b_ref
  55.0 0.0 copy-done.5
  55.0 2.7 %fwd1.1 = (bf16[8,32,416]{2,1,0:T(8,128)(2,1)S(1)}, bf16[8,32,416]{2,1,0:T(8,128)(2,1)S(1)}) custom-call(bf16[8,32,416]{2,1,0:T(8,128)(2,1)S(1)} %collective-permute-done.recv_a_ref, bf16[8,32,416]{2,1,0:T(8,128)(2,1)S(1)} %collective-permute-done.1.recv_b_ref, bf16[2,2,1,8,32,416]{5,4,3,2,1,0:T(8,128)(2,1)S(1)} %copy-done.5, ...), custom_call_target="tpu_custom_call" | custom-call | tf_op jit(solution)/shard_map/fwd1/fwd1/pallas_call | solution.py:443
  57.7 0.1 collective-permute-start.2
  57.8 5.6 %collective-permute-start.3 = (bf16[8,32,416]{2,1,0:T(8,128)(2,1)S(1)}, bf16[8,32,416]{2,1,0:T(8,128)(2,1)S(1)}, u32[]{:S(2)}, u32[]{:S(2)}) collective-permute-start(bf16[8,32,416]{2,1,0:T(8,128)(2,1)S(1)} %get-tuple-element.45), channel_id=1, source_target_pairs={{0,248},{8,0},{16,8},{24,16},{32,24},{40,32},{48,40},{56,48},{64,5... | collective-permute-start | bytes 638984 | tf_op jit(solution)/shard_map/pf1b/ppermute | solution.py:458
  63.4 0.0 collective-permute-done.8.one_ref
  63.4 3.2 %collective-permute-start.12 = (bf16[104,512]{1,0:T(8,128)(2,1)S(1)}, bf16[104,512]{1,0:T(8,128)(2,1)S(1)}, u32[]{:S(2)}, u32[]{:S(2)}) collective-permute-start(bf16[104,512]{1,0:T(8,128)(2,1)S(1)} %get-tuple-element.69), channel_id=1, source_target_pairs={{0,1},{1,2},{2,3},{3,0},{4,5},{5,6},{6,7},{7,4},{8,9},{9,10},{10,1... | collective-permute-start | bytes 319496 | tf_op jit(solution)/shard_map/xb1/ppermute | solution.py:526
  66.6 0.0 collective-permute-done.9.two_ref
  66.6 0.1 collective-permute-start.13
  66.8 0.0 collective-permute-done.10.three_ref
  66.8 1.3 %collective-permute-start.14 = (bf16[104,512]{1,0:T(8,128)(2,1)S(1)}, bf16[104,512]{1,0:T(8,128)(2,1)S(1)}, u32[]{:S(2)}, u32[]{:S(2)}) collective-permute-start(bf16[104,512]{1,0:T(8,128)(2,1)S(1)} %get-tuple-element.71), channel_id=1, source_target_pairs={{0,3},{1,0},{2,1},{3,2},{4,7},{5,4},{6,5},{7,6},{8,11},{9,8},{10,9... | collective-permute-start | bytes 319496 | tf_op jit(solution)/shard_map/xb3/ppermute | solution.py:526
  68.1 0.1 suma.1
  68.2 0.7 collective-permute-done.12.one_ref
  68.9 4.5 %collective-permute-start.11 = (bf16[52,512]{1,0:T(8,128)(2,1)S(1)}, bf16[52,512]{1,0:T(8,128)(2,1)S(1)}, u32[]{:S(2)}, u32[]{:S(2)}) collective-permute-start(bf16[52,512]{1,0:T(8,128)(2,1)S(1)} %get-tuple-element.67), channel_id=1, source_target_pairs={{0,4},{1,5},{2,6},{3,7},{4,0},{5,1},{6,2},{7,3},{8,12},{9,13},{10,... | collective-permute-start | bytes 159752 | tf_op jit(solution)/shard_map/across/ppermute | solution.py:551
  73.4 0.0 collective-permute-done.13.two_ref
  73.4 0.4 collective-permute-done.14.three_ref
  73.8 0.1 sumb.1
  73.9 0.1 collective-permute-start.15
  74.0 6.9 %collective-permute-start.16 = (bf16[52,512]{1,0:T(8,128)(2,1)S(1)}, bf16[52,512]{1,0:T(8,128)(2,1)S(1)}, u32[]{:S(2)}, u32[]{:S(2)}) collective-permute-start(bf16[52,512]{1,0:T(8,128)(2,1)S(1)} %get-tuple-element.73), channel_id=1, source_target_pairs={{0,252},{1,253},{2,254},{3,255},{4,248},{5,249},{6,250},{7,251},{8... | collective-permute-start | bytes 159752 | tf_op jit(solution)/shard_map/mirrorz/ppermute | solution.py:547
  80.9 0.0 collective-permute-done.2.recv_a_ref
  80.9 0.0 collective-permute-done.3.recv_b_ref
  80.9 3.5 %fwd2.1 = bf16[2,1,1,8,32,416]{5,4,3,2,1,0:T(8,128)(2,1)} custom-call(bf16[8,32,416]{2,1,0:T(8,128)(2,1)S(1)} %collective-permute-done.2.recv_a_ref, bf16[8,32,416]{2,1,0:T(8,128)(2,1)S(1)} %collective-permute-done.3.recv_b_ref, bf16[2,2,1,8,32,416]{5,4,3,2,1,0:T(8,128)(2,1)S(1)} %copy-done.5, bf16[25,2,416]{2,1,0:T(2,128)(2,1)S(1)} %bitcast.18, ...), custom_call_target="tpu_custom_call" | custom-call | tf_op jit(solution)/shard_map/fwd2/fwd2/pallas_call | solution.py:443
  84.4 0.0 collective-permute-done.11.far_ref
  84.4 0.0 collective-permute-done.15.cross_ref
  84.4 0.0 collective-permute-done.16.both_ref
  84.4 0.8 finish.1
  (5 shorter events, 0.0 us)
Async XLA Ops:
  0.6 1.4 %copy-start = (bf16[2,3,1,1,8,32,416]{6,5,4,3,2,1,0:T(8,128)(2,1)S(1)}, bf16[2,3,1,1,8,32,416]{6,5,4,3,2,1,0:T(8,128)(2,1)}, u32[]{:S(2)}) copy-start(bf16[2,3,1,1,8,32,416]{6,5,4,3,2,1,0:T(8,128)(2,1)} %stored_ref.3) | copy-start | bytes 3833860
  2.0 1.2 %copy-start.2 = (bf16[1,2,1,416,416]{4,3,2,1,0:T(8,128)(2,1)S(1)}, bf16[1,2,1,416,416]{4,3,2,1,0:T(8,128)(2,1)}, u32[]{:S(2)}) copy-start(bf16[1,2,1,416,416]{4,3,2,1,0:T(8,128)(2,1)} %mixing_ref.9) | copy-start | bytes 2076676
  3.2 0.8 copy-start.6
  4.0 1.0 %copy-start.8 = (bf16[2,1,1,8,32,416]{5,4,3,2,1,0:T(8,128)(2,1)S(1)}, bf16[2,1,1,8,32,416]{5,4,3,2,1,0:T(8,128)(2,1)}, u32[]{:S(2)}) copy-start(bf16[2,1,1,8,32,416]{5,4,3,2,1,0:T(8,128)(2,1)} %param.10) | copy-start | bytes 1277956
  5.0 0.7 copy-start.11
  5.7 11.9 %copy-start.3 = (bf16[1,2,1,416,416]{4,3,2,1,0:T(8,128)(2,1)S(1)}, bf16[1,2,1,416,416]{4,3,2,1,0:T(8,128)(2,1)}, u32[]{:S(2)}) copy-start(bf16[1,2,1,416,416]{4,3,2,1,0:T(8,128)(2,1)} %mixing_ref.9) | copy-start | bytes 2076676
  5.7 11.9 %copy-start.10 = (bf16[2,1,1,8,32,416]{5,4,3,2,1,0:T(8,128)(2,1)S(1)}, bf16[2,1,1,8,32,416]{5,4,3,2,1,0:T(8,128)(2,1)}, u32[]{:S(2)}) copy-start(bf16[2,1,1,8,32,416]{5,4,3,2,1,0:T(8,128)(2,1)} %refs_0_.2) | copy-start | bytes 1277956
  11.1 13.5 %collective-permute-start.4 = (bf16[8,32,416]{2,1,0:T(8,128)(2,1)S(1)}, bf16[8,32,416]{2,1,0:T(8,128)(2,1)S(1)}, u32[]{:S(2)}, u32[]{:S(2)}) collective-permute-start(bf16[8,32,416]{2,1,0:T(8,128)(2,1)S(1)} %get-tuple-element.46), channel_id=1, source_target_pairs={{0,248},{8,0},{16,8},{24,16},{32,24},{40,32},{48,40},{56,48},{64,5... | collective-permute-start | bytes 638984 | tf_op jit(solution)/shard_map/pc0a/ppermute | solution.py:458
  17.7 9.7 %collective-permute-start.5 = (bf16[8,32,416]{2,1,0:T(8,128)(2,1)S(1)}, bf16[8,32,416]{2,1,0:T(8,128)(2,1)S(1)}, u32[]{:S(2)}, u32[]{:S(2)}) collective-permute-start(bf16[8,32,416]{2,1,0:T(8,128)(2,1)S(1)} %get-tuple-element.47), channel_id=1, source_target_pairs={{0,8},{8,16},{16,24},{24,32},{32,40},{40,48},{48,56},{56,64},{64,7... | collective-permute-start | bytes 638984 | tf_op jit(solution)/shard_map/pc0b/ppermute | solution.py:458
  17.7 9.7 %copy-start.4 = (bf16[2,2,1,8,32,416]{5,4,3,2,1,0:T(8,128)(2,1)S(1)}, bf16[2,2,1,8,32,416]{5,4,3,2,1,0:T(8,128)(2,1)}, u32[]{:S(2)}) copy-start(bf16[2,2,1,8,32,416]{5,4,3,2,1,0:T(8,128)(2,1)} %loss_ref.5) | copy-start | bytes 2555908
  17.7 9.7 %copy-start.7 = (bf16[1,2,1,5,5,416]{5,1,4,3,2,0:T(2,128)(2,1)S(1)}, bf16[1,2,1,5,5,416]{5,1,4,3,2,0:T(2,128)(2,1)}, u32[]{:S(2)}) copy-start(bf16[1,2,1,5,5,416]{5,1,4,3,2,0:T(2,128)(2,1)} %param.13) | copy-start | bytes 124804
  27.4 13.7 %copy-start.1 = (bf16[2,3,1,1,8,32,416]{6,5,4,3,2,1,0:T(8,128)(2,1)S(1)}, bf16[2,3,1,1,8,32,416]{6,5,4,3,2,1,0:T(8,128)(2,1)}, u32[]{:S(2)}) copy-start(bf16[2,3,1,1,8,32,416]{6,5,4,3,2,1,0:T(8,128)(2,1)} %stored_ref.3) | copy-start | bytes 3833860
  27.4 13.7 %copy-start.9 = (bf16[2,1,1,8,32,416]{5,4,3,2,1,0:T(8,128)(2,1)S(1)}, bf16[2,1,1,8,32,416]{5,4,3,2,1,0:T(8,128)(2,1)}, u32[]{:S(2)}) copy-start(bf16[2,1,1,8,32,416]{5,4,3,2,1,0:T(8,128)(2,1)} %param.10) | copy-start | bytes 1277956
  29.7 16.7 %collective-permute-start.7 = (bf16[8,32,416]{2,1,0:T(8,128)(2,1)S(1)}, bf16[8,32,416]{2,1,0:T(8,128)(2,1)S(1)}, u32[]{:S(2)}, u32[]{:S(2)}) collective-permute-start(bf16[8,32,416]{2,1,0:T(8,128)(2,1)S(1)} %get-tuple-element.59), channel_id=1, source_target_pairs={{0,8},{8,16},{16,24},{24,32},{32,40},{40,48},{48,56},{56,64},{64,7... | collective-permute-start | bytes 638984 | tf_op jit(solution)/shard_map/pc1b/ppermute | solution.py:458
  29.8 19.2 %collective-permute-start.6 = (bf16[8,32,416]{2,1,0:T(8,128)(2,1)S(1)}, bf16[8,32,416]{2,1,0:T(8,128)(2,1)S(1)}, u32[]{:S(2)}, u32[]{:S(2)}) collective-permute-start(bf16[8,32,416]{2,1,0:T(8,128)(2,1)S(1)} %get-tuple-element.49), channel_id=1, source_target_pairs={{0,248},{8,0},{16,8},{24,16},{32,24},{40,32},{48,40},{56,48},{64,5... | collective-permute-start | bytes 638984 | tf_op jit(solution)/shard_map/pc1a/ppermute | solution.py:458
  35.4 19.5 %collective-permute-start = (bf16[8,32,416]{2,1,0:T(8,128)(2,1)S(1)}, bf16[8,32,416]{2,1,0:T(8,128)(2,1)S(1)}, u32[]{:S(2)}, u32[]{:S(2)}) collective-permute-start(bf16[8,32,416]{2,1,0:T(8,128)(2,1)S(1)} %get-tuple-element.42), channel_id=1, source_target_pairs={{0,8},{8,16},{16,24},{24,32},{32,40},{40,48},{48,56},{56,64},{64,7... | collective-permute-start | bytes 638984 | tf_op jit(solution)/shard_map/pf0a/ppermute | solution.py:458
  35.5 19.5 %collective-permute-start.1 = (bf16[8,32,416]{2,1,0:T(8,128)(2,1)S(1)}, bf16[8,32,416]{2,1,0:T(8,128)(2,1)S(1)}, u32[]{:S(2)}, u32[]{:S(2)}) collective-permute-start(bf16[8,32,416]{2,1,0:T(8,128)(2,1)S(1)} %get-tuple-element.43), channel_id=1, source_target_pairs={{0,248},{8,0},{16,8},{24,16},{32,24},{40,32},{48,40},{56,48},{64,5... | collective-permute-start | bytes 638984 | tf_op jit(solution)/shard_map/pf0b/ppermute | solution.py:458
  49.0 6.0 %copy-start.5 = (bf16[2,2,1,8,32,416]{5,4,3,2,1,0:T(8,128)(2,1)S(1)}, bf16[2,2,1,8,32,416]{5,4,3,2,1,0:T(8,128)(2,1)}, u32[]{:S(2)}) copy-start(bf16[2,2,1,8,32,416]{5,4,3,2,1,0:T(8,128)(2,1)} %new_ref.3) | copy-start | bytes 2555908
  52.1 11.3 %collective-permute-start.8 = (bf16[104,512]{1,0:T(8,128)(2,1)S(1)}, bf16[104,512]{1,0:T(8,128)(2,1)S(1)}, u32[]{:S(2)}, u32[]{:S(2)}) collective-permute-start(bf16[104,512]{1,0:T(8,128)(2,1)S(1)} %get-tuple-element.63), channel_id=1, source_target_pairs={{0,1},{1,2},{2,3},{3,0},{4,5},{5,6},{6,7},{7,4},{8,9},{9,10},{10,1... | collective-permute-start | bytes 319496 | tf_op jit(solution)/shard_map/xa1/ppermute | solution.py:526
  52.5 14.1 %collective-permute-start.9 = (bf16[104,512]{1,0:T(8,128)(2,1)S(1)}, bf16[104,512]{1,0:T(8,128)(2,1)S(1)}, u32[]{:S(2)}, u32[]{:S(2)}) collective-permute-start(bf16[104,512]{1,0:T(8,128)(2,1)S(1)} %get-tuple-element.64), channel_id=1, source_target_pairs={{0,2},{1,3},{2,0},{3,1},{4,6},{5,7},{6,4},{7,5},{8,10},{9,11},{10,... | collective-permute-start | bytes 319496 | tf_op jit(solution)/shard_map/xa2/ppermute | solution.py:526
  55.0 11.8 %collective-permute-start.10 = (bf16[104,512]{1,0:T(8,128)(2,1)S(1)}, bf16[104,512]{1,0:T(8,128)(2,1)S(1)}, u32[]{:S(2)}, u32[]{:S(2)}) collective-permute-start(bf16[104,512]{1,0:T(8,128)(2,1)S(1)} %get-tuple-element.65), channel_id=1, source_target_pairs={{0,3},{1,0},{2,1},{3,2},{4,7},{5,4},{6,5},{7,6},{8,11},{9,8},{10,9... | collective-permute-start | bytes 319496 | tf_op jit(solution)/shard_map/xa3/ppermute | solution.py:526
  57.7 23.2 %collective-permute-start.2 = (bf16[8,32,416]{2,1,0:T(8,128)(2,1)S(1)}, bf16[8,32,416]{2,1,0:T(8,128)(2,1)S(1)}, u32[]{:S(2)}, u32[]{:S(2)}) collective-permute-start(bf16[8,32,416]{2,1,0:T(8,128)(2,1)S(1)} %get-tuple-element.44), channel_id=1, source_target_pairs={{0,8},{8,16},{16,24},{24,32},{32,40},{40,48},{48,56},{56,64},{64,7... | collective-permute-start | bytes 638984 | tf_op jit(solution)/shard_map/pf1a/ppermute | solution.py:458
  57.8 23.1 %collective-permute-start.3 = (bf16[8,32,416]{2,1,0:T(8,128)(2,1)S(1)}, bf16[8,32,416]{2,1,0:T(8,128)(2,1)S(1)}, u32[]{:S(2)}, u32[]{:S(2)}) collective-permute-start(bf16[8,32,416]{2,1,0:T(8,128)(2,1)S(1)} %get-tuple-element.45), channel_id=1, source_target_pairs={{0,248},{8,0},{16,8},{24,16},{32,24},{40,32},{48,40},{56,48},{64,5... | collective-permute-start | bytes 638984 | tf_op jit(solution)/shard_map/pf1b/ppermute | solution.py:458
  63.4 5.5 %collective-permute-start.12 = (bf16[104,512]{1,0:T(8,128)(2,1)S(1)}, bf16[104,512]{1,0:T(8,128)(2,1)S(1)}, u32[]{:S(2)}, u32[]{:S(2)}) collective-permute-start(bf16[104,512]{1,0:T(8,128)(2,1)S(1)} %get-tuple-element.69), channel_id=1, source_target_pairs={{0,1},{1,2},{2,3},{3,0},{4,5},{5,6},{6,7},{7,4},{8,9},{9,10},{10,1... | collective-permute-start | bytes 319496 | tf_op jit(solution)/shard_map/xb1/ppermute | solution.py:526
  66.6 6.8 %collective-permute-start.13 = (bf16[104,512]{1,0:T(8,128)(2,1)S(1)}, bf16[104,512]{1,0:T(8,128)(2,1)S(1)}, u32[]{:S(2)}, u32[]{:S(2)}) collective-permute-start(bf16[104,512]{1,0:T(8,128)(2,1)S(1)} %get-tuple-element.70), channel_id=1, source_target_pairs={{0,2},{1,3},{2,0},{3,1},{4,6},{5,7},{6,4},{7,5},{8,10},{9,11},{10,... | collective-permute-start | bytes 319496 | tf_op jit(solution)/shard_map/xb2/ppermute | solution.py:526
  66.8 7.1 %collective-permute-start.14 = (bf16[104,512]{1,0:T(8,128)(2,1)S(1)}, bf16[104,512]{1,0:T(8,128)(2,1)S(1)}, u32[]{:S(2)}, u32[]{:S(2)}) collective-permute-start(bf16[104,512]{1,0:T(8,128)(2,1)S(1)} %get-tuple-element.71), channel_id=1, source_target_pairs={{0,3},{1,0},{2,1},{3,2},{4,7},{5,4},{6,5},{7,6},{8,11},{9,8},{10,9... | collective-permute-start | bytes 319496 | tf_op jit(solution)/shard_map/xb3/ppermute | solution.py:526
  68.9 15.5 %collective-permute-start.11 = (bf16[52,512]{1,0:T(8,128)(2,1)S(1)}, bf16[52,512]{1,0:T(8,128)(2,1)S(1)}, u32[]{:S(2)}, u32[]{:S(2)}) collective-permute-start(bf16[52,512]{1,0:T(8,128)(2,1)S(1)} %get-tuple-element.67), channel_id=1, source_target_pairs={{0,4},{1,5},{2,6},{3,7},{4,0},{5,1},{6,2},{7,3},{8,12},{9,13},{10,... | collective-permute-start | bytes 159752 | tf_op jit(solution)/shard_map/across/ppermute | solution.py:551
  73.9 10.5 %collective-permute-start.15 = (bf16[52,512]{1,0:T(8,128)(2,1)S(1)}, bf16[52,512]{1,0:T(8,128)(2,1)S(1)}, u32[]{:S(2)}, u32[]{:S(2)}) collective-permute-start(bf16[52,512]{1,0:T(8,128)(2,1)S(1)} %get-tuple-element.72), channel_id=1, source_target_pairs={{0,248},{8,240},{16,232},{24,224},{32,216},{40,208},{48,200},{56,1... | collective-permute-start | bytes 159752 | tf_op jit(solution)/shard_map/mirror/ppermute | solution.py:545
  74.0 10.4 %collective-permute-start.16 = (bf16[52,512]{1,0:T(8,128)(2,1)S(1)}, bf16[52,512]{1,0:T(8,128)(2,1)S(1)}, u32[]{:S(2)}, u32[]{:S(2)}) collective-permute-start(bf16[52,512]{1,0:T(8,128)(2,1)S(1)} %get-tuple-element.73), channel_id=1, source_target_pairs={{0,252},{1,253},{2,254},{3,255},{4,248},{5,249},{6,250},{7,251},{8... | collective-permute-start | bytes 159752 | tf_op jit(solution)/shard_map/mirrorz/ppermute | solution.py:547
